TPU v7x, 32 devices: a whole 2x2x4 slice. The times are simulated.
32 devices in a mesh: group: 4 (over x, core), ep: 8 (over z, y).
Axes of the slice: x: 2, y: 2, z: 4, core: 2. Of those that a mesh axis runs over, the one named last changes fastest.
Arguments:
- tokens: bfloat16 [4096, 4096], P(('group', 'ep')), may hold values from -6 to 6
- out_grad: bfloat16 [4096, 4096], P(('group', 'ep')), may hold values from -6 to 6
- routes: int32 [4096, 2], P(('group', 'ep')), may hold values from 0 to 63, all different within a row; in each aligned block of 128 rows (0 to 127, 128 to 255, ...) at most 5 rows name the same one
- gate_probs: float32 [4096, 2], P(('group', 'ep')), may hold values from 0.1 to 1
- hot: int32 [1], replicated, may hold values from 0 to 65535
- gate_weight: bfloat16 [4, 4096, 11008], P('group', None, 'ep'), may hold values from -0.09375 to 0.09375
- up_weight: bfloat16 [4, 4096, 11008], P('group', None, 'ep'), may hold values from -0.09375 to 0.09375
- down_weight: bfloat16 [4, 11008, 4096], P('group', 'ep'), may hold values from -0.0546875 to 0.0546875
Outputs:
- tokens_grad: bfloat16 [4096, 4096], P(('group', 'ep'))
- gate_weight_grad: bfloat16 [4, 4096, 11008], P('group', None, 'ep')
- up_weight_grad: bfloat16 [4, 4096, 11008], P('group', None, 'ep')
- down_weight_grad: bfloat16 [4, 11008, 4096], P('group', 'ep')
Inputs may be any that keep to these rules, and one draw needn't show every extreme that they name: `routes`: each row names two different experts. Among the 128 rows of one device, at most 5 name the same expert.
All inputs are finite; a program needn't handle non-finite values.
Results may differ from a plain program's by a relative error of at most 0.024.
Values may be sent and summed in bfloat16 or wider, within the bound.
No kernel may reach another device: no remote copies, remote signals or barrier semaphores. Data moves between devices by JAX's collectives and lax.ppermute only.
A program may use at most 448 MiB of HBM per device.

v0:
```python
import jax
import jax.numpy as jnp
from jax import lax
from jax.sharding import PartitionSpec as P

CAP = 5
COLD_CAP = 3


def slot_map(route_block, prob_block, experts, capacity):
    expert_index = jnp.arange(experts, dtype=jnp.int32)
    named_hits = route_block[None, :, :] == expert_index[:, None, None]
    weight_sum = jnp.sum(jnp.where(named_hits, prob_block[None, :, :], 0.0), axis=2)
    chosen = jnp.any(named_hits, axis=2).astype(jnp.int32)
    position = jnp.cumsum(chosen, axis=1) - 1
    slot_index = jnp.arange(capacity, dtype=jnp.int32)
    onehot = (
        (position[:, None, :] == slot_index[None, :, None]) & (chosen[:, None, :] == 1)
    ).astype(jnp.float32)
    slot_weight = jnp.sum(onehot * weight_sum[:, None, :], axis=2)
    return (onehot, slot_weight)


def contract(left, right, left_dim, right_dim):
    return lax.dot_general(
        left, right, (((left_dim,), (right_dim,)), ((), ())), preferred_element_type=jnp.float32
    )


def settle(partial_term, rounded):
    narrowed = lax.optimization_barrier(partial_term.astype(jnp.bfloat16)).astype(jnp.float32)
    return jnp.where(rounded, narrowed, partial_term)


def expert_signals(token_rows, signal_rows, gate_w, up_w, down_w):
    gate_pre = jnp.dot(token_rows, gate_w, preferred_element_type=jnp.float32)
    up_pre = jnp.dot(token_rows, up_w, preferred_element_type=jnp.float32)
    logistic = jax.nn.sigmoid(gate_pre)
    swished = gate_pre * logistic
    hidden = (swished * up_pre).astype(jnp.bfloat16)
    hidden_grad = contract(signal_rows, down_w, 1, 1)
    gate_signal = (hidden_grad * up_pre * logistic * (1.0 + gate_pre * (1.0 - logistic))).astype(
        jnp.bfloat16
    )
    up_signal = (hidden_grad * swished).astype(jnp.bfloat16)
    token_grad = contract(gate_signal, gate_w, 1, 1) + contract(up_signal, up_w, 1, 1)
    return (hidden, gate_signal, up_signal, token_grad)


def weight_terms(token_rows, signal_rows, hidden, gate_signal, up_signal):
    return (
        contract(token_rows, gate_signal, 0, 0),
        contract(token_rows, up_signal, 0, 0),
        contract(hidden, signal_rows, 0, 0),
    )


def owner_backward(token_all, signal_all, gate_w, up_w, down_w, rounded):
    slices, groups, slot_count, width = token_all.shape
    hidden, gate_signal, up_signal, token_grad = expert_signals(
        token_all.reshape(-1, width), signal_all.reshape(-1, width), gate_w, up_w, down_w
    )
    inner_width = hidden.shape[1]
    hidden_g = hidden.reshape(slices, groups, slot_count, inner_width)
    gate_g = gate_signal.reshape(slices, groups, slot_count, inner_width)
    up_g = up_signal.reshape(slices, groups, slot_count, inner_width)
    totals = None
    for source in range(groups):
        pieces = weight_terms(
            token_all[:, source].reshape(-1, width),
            signal_all[:, source].reshape(-1, width),
            hidden_g[:, source].reshape(-1, inner_width),
            gate_g[:, source].reshape(-1, inner_width),
            up_g[:, source].reshape(-1, inner_width),
        )
        pieces = tuple((settle(piece, rounded) for piece in pieces))
        totals = (
            pieces
            if totals is None
            else tuple((total + piece for total, piece in zip(totals, pieces)))
        )
    return (totals, token_grad)


def per_device(tokens, out_grad, routes, gate_probs, hot, gate_weight, up_weight, down_weight):
    owned = gate_weight.shape[0]
    groups = lax.axis_size("group")
    slices = lax.axis_size("ep")
    experts = owned * groups
    width = tokens.shape[1]
    onehot, slot_weight = slot_map(routes, gate_probs, experts, CAP)
    hot_id = jnp.remainder(hot[0], experts)
    is_hot = jnp.arange(experts, dtype=jnp.int32) == hot_id
    slot_ids = jnp.arange(CAP, dtype=jnp.int32)
    retained = is_hot[:, None] | (slot_ids[None, :] < COLD_CAP)
    slot_count = CAP
    retained_f = retained.astype(jnp.float32)
    cold_pick = onehot * retained_f[:, :, None]
    cold_weight = slot_weight * retained_f
    picker = cold_pick.astype(jnp.bfloat16)
    token_slots = jnp.einsum(
        "est,td->esd", picker, tokens, preferred_element_type=jnp.float32
    ).astype(jnp.bfloat16)
    picked = jnp.einsum("est,td->esd", picker, out_grad, preferred_element_type=jnp.float32)
    signal_slots = (cold_weight[:, :, None] * picked).astype(jnp.bfloat16)
    token_slots = token_slots.reshape(1, groups, owned, slot_count, width)
    signal_slots = signal_slots.reshape(1, groups, owned, slot_count, width)
    token_owned, signal_owned = (
        lax.all_to_all(token_slots, "group", split_axis=1, concat_axis=1, tiled=True),
        lax.all_to_all(signal_slots, "group", split_axis=1, concat_axis=1, tiled=True),
    )
    token_all, signal_all = (
        lax.all_gather(token_owned, "ep", axis=0, tiled=True),
        lax.all_gather(signal_owned, "ep", axis=0, tiled=True),
    )
    own_group = lax.axis_index("group")
    mine_hot = own_group * owned + 0 == hot_id
    totals, token_grad = owner_backward(
        token_all[:, :, 0],
        signal_all[:, :, 0],
        gate_weight[0],
        up_weight[0],
        down_weight[0],
        mine_hot,
    )
    totals_list = [totals]
    grad_parts = token_grad.reshape(slices, groups, 1, slot_count, width)
    summed = lax.psum_scatter(
        grad_parts.astype(jnp.bfloat16), "ep", scatter_dimension=0, tiled=True
    ).astype(jnp.float32)
    returned = lax.all_to_all(
        summed.astype(jnp.bfloat16), "group", split_axis=1, concat_axis=1, tiled=True
    ).astype(summed.dtype)
    grad_slots = returned.reshape(experts, slot_count, width)
    back_total = jnp.einsum(
        "est,esd->td",
        cold_pick,
        grad_slots,
        precision=lax.Precision.HIGHEST,
        preferred_element_type=jnp.float32,
    )
    tokens_grad = back_total.astype(jnp.bfloat16)
    gate_grad = jnp.stack([totals[0] for totals in totals_list]).astype(jnp.bfloat16)
    up_grad = jnp.stack([totals[1] for totals in totals_list]).astype(jnp.bfloat16)
    down_grad = jnp.stack([totals[2] for totals in totals_list]).astype(jnp.bfloat16)
    return (tokens_grad, gate_grad, up_grad, down_grad)


def solution(mesh):
    in_specs = (
        P(("group", "ep"), None),
        P(("group", "ep"), None),
        P(("group", "ep"), None),
        P(("group", "ep"), None),
        P(),
        P("group", None, "ep"),
        P("group", None, "ep"),
        P("group", "ep", None),
    )
    out_specs = (
        P(("group", "ep"), None),
        P("group", None, "ep"),
        P("group", None, "ep"),
        P("group", "ep", None),
    )
    return jax.shard_map(
        per_device, mesh=mesh, in_specs=in_specs, out_specs=out_specs, check_vma=False
    )
```

profile of v0, /device:TPU:0, one launch (start us, length us, event | category | flops | bytes accessed | tf_op | source)
XLA Modules:
  0.0 455.2 jit_solution(7165123474316122006)
XLA Ops:
  9.4 10.0 %all_to_all.15 = bf16[1,4,1,5,4096]{4,3,2,0,1:T(8,128)(2,1)S(1)} all-to-all(bf16[1,4,1,5,4096]{4,3,2,0,1:T(8,128)(2,1)S(1)} %fusion.33), channel_id=1, replica_groups=mesh['group'=4,'ep'=8] {'group'}, dimensions={1} | all-to-all | bytes 327680 | tf_op jit(solution)/shard_map/all_to_all | solution.py:109
  22.8 8.4 %all_to_all.16 = bf16[1,4,1,5,4096]{4,3,2,0,1:T(8,128)(2,1)S(1)} all-to-all(bf16[1,4,1,5,4096]{4,3,2,0,1:T(8,128)(2,1)S(1)} %fusion.34), channel_id=1, replica_groups=mesh['group'=4,'ep'=8] {'group'}, dimensions={1} | all-to-all | bytes 327680 | tf_op jit(solution)/shard_map/all_to_all | solution.py:110
  32.1 30.5 %all-gather.5.cloned.1.call-done = bf16[8,4,1,5,4096]{4,1,3,2,0:T(4,128)(2,1)} async-done(((bf16[1,4,1,5,4096]{4,1,3,2,0:T(4,128)(2,1)}), bf16[8,4,1,5,4096]{4,1,3,2,0:T(4,128)(2,1)}) %all-gather.5.cloned.1.call-update) | async-done | bytes 1310736 | tf_op jit(solution)/shard_map/all_gather | solution.py:113
  66.1 39.9 %all-gather.3.cloned.1.call-done = bf16[8,4,1,5,4096]{4,1,3,2,0:T(4,128)(2,1)} async-done(((bf16[1,4,1,5,4096]{4,1,3,2,0:T(4,128)(2,1)}), bf16[8,4,1,5,4096]{4,1,3,2,0:T(4,128)(2,1)}) %all-gather.3.cloned.1.call-update) | async-done | bytes 1310736 | tf_op jit(solution)/shard_map/all_gather | solution.py:114
  109.7 8.6 %fusion.17 = f32[160,1376]{1,0:T(8,128)S(1)} fusion(bf16[160,4096]{1,0:T(8,128)(2,1)} %reshape_squeeze.5, bf16[1,4096,1376]{1,2,0:T(8,128)(2,1)} %param.13), kind=kOutput, calls=%fused_computation.41 | convolution fusion | flops 1803550720 | bytes 13463552 | tf_op jit(solution)/shard_map/dot_general | solution.py:36
  118.3 8.2 %fusion.23 = f32[160,1376]{1,0:T(8,128)S(1)} fusion(bf16[160,4096]{1,0:T(8,128)(2,1)S(1)} %copy-done.4, bf16[1,1376,4096]{2,1,0:T(8,128)(2,1)} %param.15), kind=kOutput, calls=%fused_computation.47 | convolution fusion | flops 1803550720 | bytes 13463552 | tf_op jit(solution)/shard_map/dot_general | solution.py:25
  126.6 9.3 %multiply_convert_fusion = (bf16[160,1376]{1,0:T(8,128)(2,1)}, bf16[160,1376]{1,0:T(8,128)(2,1)S(1)}, bf16[160,1376]{1,0:T(8,128)(2,1)}) fusion(f32[160,1376]{1,0:T(8,128)S(1)} %fusion.17, f32[160,1376]{1,0:T(8,128)S(1)} %fusion.23, bf16[160,4096]{1,0:T(8,128)(2,1)S(1)} %copy-done.3, bf16[1,4096,1376]{1,2,0:T(8,128)(2,1)} %param.14), kind=kOutput, calls=%fused_computation.62 | convolution fusion | flops 1806853120 | bytes 15665152 | tf_op jit(solution)/shard_map/dot_general | solution.py:37
  135.9 3.8 fusion.15
  142.1 13.2 %bitcast_convert_fusion.8 = (bf16[4096,1376]{0,1:T(8,128)(2,1)}, f32[4096,1376,1]{0,1,2:T(8,128)}) fusion(bf16[8,4,5,1376]{3,2,1,0:T(8,128)(2,1)S(1)} %reshape.194, bf16[8,4,5,4096]{3,2,0,1:T(8,128)(2,1)S(1)} %bitcast.298), kind=kOutput, calls=%fused_computation.25 | convolution fusion | flops 456523776 | bytes 34521088 | tf_op jit(solution)/shard_map/dot_general | solution.py:25
  155.3 13.0 %bitcast_convert_fusion.9 = (bf16[4096,1376]{0,1:T(8,128)(2,1)}, f32[4096,1376,1]{0,1,2:T(8,128)}) fusion(bf16[8,4,5,1376]{3,2,1,0:T(8,128)(2,1)S(1)} %reshape.194, bf16[8,4,5,4096]{3,2,0,1:T(8,128)(2,1)S(1)} %bitcast.299), kind=kOutput, calls=%fused_computation.29 | convolution fusion | flops 456523776 | bytes 34521088 | tf_op jit(solution)/shard_map/dot_general | solution.py:25
  168.3 13.0 %bitcast_convert_fusion.10 = (bf16[4096,1376]{0,1:T(8,128)(2,1)}, f32[4096,1376,1]{0,1,2:T(8,128)}) fusion(bf16[8,4,5,1376]{3,2,1,0:T(8,128)(2,1)S(1)} %reshape.194, bf16[8,4,5,4096]{3,2,0,1:T(8,128)(2,1)S(1)} %bitcast.300), kind=kOutput, calls=%fused_computation.32 | convolution fusion | flops 456523776 | bytes 34521088 | tf_op jit(solution)/shard_map/dot_general | solution.py:25
  181.3 12.6 %bitcast_convert_fusion.11 = (bf16[4096,1376]{0,1:T(8,128)(2,1)}, f32[4096,1376,1]{0,1,2:T(8,128)}) fusion(bf16[8,4,5,1376]{3,2,1,0:T(8,128)(2,1)S(1)} %reshape.194, bf16[8,4,5,4096]{3,2,0,1:T(8,128)(2,1)S(1)} %bitcast.301), kind=kOutput, calls=%fused_computation.35 | convolution fusion | flops 456523776 | bytes 34521088 | tf_op jit(solution)/shard_map/dot_general | solution.py:25
  195.1 12.7 %bitcast_convert_fusion.4 = (bf16[4096,1376]{0,1:T(8,128)(2,1)}, f32[4096,1376,1]{0,1,2:T(8,128)}) fusion(bf16[8,4,5,1376]{3,2,1,0:T(8,128)(2,1)S(1)} %reshape.202, bf16[8,4,5,4096]{3,2,0,1:T(8,128)(2,1)S(1)} %bitcast.302), kind=kOutput, calls=%fused_computation.13 | convolution fusion | flops 456523776 | bytes 34521088 | tf_op jit(solution)/shard_map/dot_general | solution.py:25
  207.8 12.8 %bitcast_convert_fusion.5 = (bf16[4096,1376]{0,1:T(8,128)(2,1)}, f32[4096,1376,1]{0,1,2:T(8,128)}) fusion(bf16[8,4,5,1376]{3,2,1,0:T(8,128)(2,1)S(1)} %reshape.202, bf16[8,4,5,4096]{3,2,0,1:T(8,128)(2,1)S(1)} %bitcast.303), kind=kOutput, calls=%fused_computation.17 | convolution fusion | flops 456523776 | bytes 34521088 | tf_op jit(solution)/shard_map/dot_general | solution.py:25
  220.6 13.1 %bitcast_convert_fusion.6 = (bf16[4096,1376]{0,1:T(8,128)(2,1)}, f32[4096,1376,1]{0,1,2:T(8,128)}) fusion(bf16[8,4,5,1376]{3,2,1,0:T(8,128)(2,1)S(1)} %reshape.202, bf16[8,4,5,4096]{3,2,0,1:T(8,128)(2,1)S(1)} %bitcast.304), kind=kOutput, calls=%fused_computation.20 | convolution fusion | flops 456523776 | bytes 34521088 | tf_op jit(solution)/shard_map/dot_general | solution.py:25
  233.7 12.7 %bitcast_convert_fusion.7 = (bf16[4096,1376]{0,1:T(8,128)(2,1)}, f32[4096,1376,1]{0,1,2:T(8,128)}) fusion(bf16[8,4,5,1376]{3,2,1,0:T(8,128)(2,1)S(1)} %reshape.202, bf16[8,4,5,4096]{3,2,0,1:T(8,128)(2,1)S(1)} %bitcast.305), kind=kOutput, calls=%fused_computation.23 | convolution fusion | flops 456523776 | bytes 34521088 | tf_op jit(solution)/shard_map/dot_general | solution.py:25
  246.4 3.3 fusion.28
  253.5 12.9 %bitcast_convert_fusion = (bf16[1376,4096]{1,0:T(8,128)(2,1)}, f32[1376,4096,1]{1,0,2:T(8,128)}) fusion(bf16[8,4,5,4096]{3,0,2,1:T(8,128)(2,1)S(1)} %bitcast.308, bf16[8,1,5,1376]{3,2,1,0:T(8,128)(2,1)S(1)} %get-tuple-element.10), kind=kOutput, calls=%fused_computation.1 | convolution fusion | flops 456523776 | bytes 34324480 | tf_op jit(solution)/shard_map/dot_general | solution.py:25
  266.3 91.3 %fusion.12 = (bf16[1,4096,1376]{1,2,0:T(8,128)(2,1)}, bf16[1,4096,1376]{1,2,0:T(8,128)(2,1)}) fusion(f32[4096,1376,1]{0,1,2:T(8,128)} %get-tuple-element.14, bf16[4096,1376]{0,1:T(8,128)(2,1)} %get-tuple-element.13, f32[4096,1376,1]{0,1,2:T(8,128)} %get-tuple-element.16, bf16[4096,1376]{0,1:T(8,128)(2,1)} %get-tuple-element.15, ...), kind=kLoop, calls=%fused_computation.36 | loop fusion | flops 135266304 | bytes 293076992 | tf_op jit(solution)/shard_map/convert_element_type | solution.py:143
  357.7 13.1 %bitcast_convert_fusion.1 = (bf16[1376,4096]{1,0:T(8,128)(2,1)}, f32[1376,4096,1]{1,0,2:T(8,128)}) fusion(bf16[8,4,5,4096]{3,0,2,1:T(8,128)(2,1)S(1)} %bitcast.309, bf16[8,1,5,1376]{3,2,1,0:T(8,128)(2,1)S(1)} %get-tuple-element.8), kind=kOutput, calls=%fused_computation.5 | convolution fusion | flops 456523776 | bytes 34324480 | tf_op jit(solution)/shard_map/dot_general | solution.py:25
  370.8 12.7 %bitcast_convert_fusion.2 = (bf16[1376,4096]{1,0:T(8,128)(2,1)}, f32[1376,4096,1]{1,0,2:T(8,128)}) fusion(bf16[8,4,5,4096]{3,0,2,1:T(8,128)(2,1)S(1)} %bitcast.310, bf16[8,1,5,1376]{3,2,1,0:T(8,128)(2,1)S(1)} %get-tuple-element.9), kind=kOutput, calls=%fused_computation.8 | convolution fusion | flops 456523776 | bytes 34324480 | tf_op jit(solution)/shard_map/dot_general | solution.py:25
  383.5 12.6 %bitcast_convert_fusion.3 = (bf16[1376,4096]{1,0:T(8,128)(2,1)}, f32[1376,4096,1]{1,0,2:T(8,128)}) fusion(bf16[8,4,5,4096]{3,0,2,1:T(8,128)(2,1)S(1)} %bitcast.311, bf16[8,1,5,1376]{3,2,1,0:T(8,128)(2,1)S(1)} %get-tuple-element.7), kind=kOutput, calls=%fused_computation.11 | convolution fusion | flops 456523776 | bytes 34324480 | tf_op jit(solution)/shard_map/dot_general | solution.py:25
  396.1 3.4 all-to-all-start.2
  399.6 46.8 %fusion.14 = bf16[1,1376,4096]{2,1,0:T(8,128)(2,1)} fusion(f32[1376,4096,1]{1,0,2:T(8,128)} %get-tuple-element.30, bf16[1376,4096]{1,0:T(8,128)(2,1)} %get-tuple-element.29, f32[1376,4096,1]{1,0,2:T(8,128)} %get-tuple-element.32, bf16[1376,4096]{1,0:T(8,128)(2,1)} %get-tuple-element.31, f32[1376,4096,1]{1,0,2:T(8,128)} %get-tuple-element.34, ...), kind=kLoop, calls=%fused_computation.38 | loop fusion | flops 67633152 | bytes 146538496 | tf_op jit(solution)/shard_map/convert_element_type | solution.py:145
  (80 shorter events, 22.2 us)
Async XLA Ops:
  7.2 55.4 %all-gather.5.cloned.1.call-start = ((), (), s32[]{:S(2)}) async-start(), calls=%async_computation.5 | async-start | bytes 1474560 | tf_op jit(solution)/shard_map/all_gather | solution.py:113
  8.7 23.3 %copy-start.14 = (pred[4,128]{1,0:T(4,128)(4,1)}, pred[4,128]{1,0:T(4,128)(4,1)S(1)}, u32[]{:S(2)}) copy-start(pred[4,128]{1,0:T(4,128)(4,1)S(1)} %get-tuple-element.11) | copy-start | bytes 1540
  9.0 23.0 %copy-start.10 = (s32[4,128]{1,0:T(4,128)}, s32[4,128]{1,0:T(4,128)S(1)}, u32[]{:S(2)}) copy-start(s32[4,128]{1,0:T(4,128)S(1)} %broadcast_add_fusion) | copy-start | bytes 6148
  9.1 23.0 %copy-start.12 = (f32[4,5]{1,0:T(4,128)}, f32[4,5]{1,0:T(4,128)S(1)}, u32[]{:S(2)}) copy-start(f32[4,5]{1,0:T(4,128)S(1)} %or_convert_fusion) | copy-start | bytes 244
  20.3 85.7 %all-gather.3.cloned.1.call-start = ((), (), s32[]{:S(2)}) async-start(), calls=%async_computation.4 | async-start | bytes 1474560 | tf_op jit(solution)/shard_map/all_gather | solution.py:114
  32.0 364.1 %reduce-scatter.2.cloned.1.call-start = ((), (), s32[]{:S(2)}) async-start(), calls=%async_computation.6 | async-start | bytes 2359296 | tf_op jit(solution)/shard_map/reduce_scatter | solution.py:128
  109.7 8.6 %copy-start.4 = (bf16[160,4096]{1,0:T(8,128)(2,1)S(1)}, bf16[160,4096]{1,0:T(8,128)(2,1)}, u32[]{:S(2)}) copy-start(bf16[160,4096]{1,0:T(8,128)(2,1)} %reshape_squeeze.4) | copy-start | bytes 3932164
  109.7 16.9 %copy-start.3 = (bf16[160,4096]{1,0:T(8,128)(2,1)S(1)}, bf16[160,4096]{1,0:T(8,128)(2,1)}, u32[]{:S(2)}) copy-start(bf16[160,4096]{1,0:T(8,128)(2,1)} %reshape_squeeze.5) | copy-start | bytes 3932164
  118.3 17.6 %slice-start = ((s8[11272192]{0:T(1024)(128)(4,1)}), s8[4194304]{0:T(1024)(128)(4,1)S(1)}, s32[]{:S(2)}) async-start(s8[11272192]{0:T(1024)(128)(4,1)} %bitcast.296), calls=%async_computation.7 | async-start | bytes 8388608
  118.3 17.6 %slice-start.1 = ((s8[11272192]{0:T(1024)(128)(4,1)}), s8[4194304]{0:T(1024)(128)(4,1)S(1)}, s32[]{:S(2)}) async-start(s8[11272192]{0:T(1024)(128)(4,1)} %bitcast.296), calls=%async_computation.8 | async-start | bytes 8388608
  126.6 9.3 %slice-start.2 = ((s8[11272192]{0:T(1024)(128)(4,1)}), s8[2883584]{0:T(1024)(128)(4,1)S(1)}, s32[]{:S(2)}) async-start(s8[11272192]{0:T(1024)(128)(4,1)} %bitcast.296), calls=%async_computation.9 | async-start | bytes 5767168
  220.6 25.8 %slice-start.3 = ((s8[11272192]{0:T(1024)(128)(4,1)}), s8[4194304]{0:T(1024)(128)(4,1)S(1)}, s32[]{:S(2)}) async-start(s8[11272192]{0:T(1024)(128)(4,1)} %bitcast.306), calls=%async_computation.10 | async-start | bytes 8388608
  220.6 25.8 %slice-start.4 = ((s8[11272192]{0:T(1024)(128)(4,1)}), s8[4194304]{0:T(1024)(128)(4,1)S(1)}, s32[]{:S(2)}) async-start(s8[11272192]{0:T(1024)(128)(4,1)} %bitcast.306), calls=%async_computation.11 | async-start | bytes 8388608
  233.7 12.7 %slice-start.5 = ((s8[11272192]{0:T(1024)(128)(4,1)}), s8[2883584]{0:T(1024)(128)(4,1)S(1)}, s32[]{:S(2)}) async-start(s8[11272192]{0:T(1024)(128)(4,1)} %bitcast.306), calls=%async_computation.12 | async-start | bytes 5767168
  233.7 12.7 %copy-start.2 = (f32[160,4096]{1,0:T(8,128)S(1)}, f32[160,4096]{1,0:T(8,128)}, u32[]{:S(2)}) copy-start(f32[160,4096]{1,0:T(8,128)} %fusion.15) | copy-start | bytes 7864324
  233.7 12.7 %copy-start.6 = (bf16[160,1376]{1,0:T(8,128)(2,1)S(1)}, bf16[160,1376]{1,0:T(8,128)(2,1)}, u32[]{:S(2)}) copy-start(bf16[160,1376]{1,0:T(8,128)(2,1)} %get-tuple-element.6) | copy-start | bytes 1320964
  246.4 6.3 %copy-start.5 = (bf16[8,4,1,5,4096]{4,1,3,2,0:T(4,128)(2,1)S(1)}, bf16[8,4,1,5,4096]{4,1,3,2,0:T(4,128)(2,1)}, u32[]{:S(2)}) copy-start(bf16[8,4,1,5,4096]{4,1,3,2,0:T(4,128)(2,1)} %all-gather.3.cloned.1.call-done) | copy-start | bytes 3932164
  253.5 12.9 %copy-start.7 = (bf16[8,4,1,5,4096]{4,0,3,1,2:T(8,128)(2,1)}, bf16[8,4,1,5,4096]{4,0,3,1,2:T(8,128)(2,1)S(1)}, u32[]{:S(2)}) copy-start(bf16[8,4,1,5,4096]{4,0,3,1,2:T(8,128)(2,1)S(1)} %copy.141) | copy-start | bytes 3932164
  266.3 91.3 %copy-start.8 = (bf16[8,4,1,5,4096]{4,0,3,1,2:T(8,128)(2,1)S(1)}, bf16[8,4,1,5,4096]{4,0,3,1,2:T(8,128)(2,1)}, u32[]{:S(2)}) copy-start(bf16[8,4,1,5,4096]{4,0,3,1,2:T(8,128)(2,1)} %copy-done.7) | copy-start | bytes 3932164
  396.1 50.3 %all-to-all-start.2 = ((bf16[1,4,1,5,4096]{4,3,2,0,1:T(8,128)(2,1)}), bf16[1,4,1,5,4096]{4,3,2,0,1:T(8,128)(2,1)S(1)}, u32[]{:S(2)}, u32[]{:S(2)}) async-start(bf16[1,4,1,5,4096]{4,3,2,0,1:T(8,128)(2,1)} %bitcast.312), calls=%async_computation.3 | async-start | bytes 524288 | tf_op jit(solution)/shard_map/all_to_all | solution.py:131
  399.5 46.9 %copy-start.11 = (s32[4,128]{1,0:T(4,128)S(1)}, s32[4,128]{1,0:T(4,128)}, u32[]{:S(2)}) copy-start(s32[4,128]{1,0:T(4,128)} %copy-done.10) | copy-start | bytes 6148
  399.5 46.9 %copy-start.13 = (f32[4,5]{1,0:T(4,128)S(1)}, f32[4,5]{1,0:T(4,128)}, u32[]{:S(2)}) copy-start(f32[4,5]{1,0:T(4,128)} %copy-done.12) | copy-start | bytes 244
  399.5 46.9 %copy-start.15 = (pred[4,128]{1,0:T(4,128)(4,1)S(1)}, pred[4,128]{1,0:T(4,128)(4,1)}, u32[]{:S(2)}) copy-start(pred[4,128]{1,0:T(4,128)(4,1)} %copy-done.14) | copy-start | bytes 1540
  399.5 49.0 %copy-start.1 = (bf16[128,4096]{1,0:T(8,128)(2,1)S(1)}, bf16[128,4096]{1,0:T(8,128)(2,1)}, u32[]{:S(2)}) copy-start(bf16[128,4096]{1,0:T(8,128)(2,1)} %param.8) | copy-start | bytes 3145732
  (2 other events, 8.0 us)
Sparse Core Ops, SparseCore 0:
  20.4 42.1 all-gather.4
  65.3 40.6 all-gather.2
  252.6 67.0 reduce-scatter.1
where the time goes:
time: 459 us; the launch traced here: 455 us
  matrix products  192 us (42%)
  other arithmetic  140 us (31%)
  waiting for transfers between devices  70.4 us (15%)
  blocking collectives  18.4 us (4%)
  local copies, waits for them, and re-layouts  16.1 us (4%)
  between operations  15 us (3%)
    dot_general x15, matrix products, contract(): lax.dot_general(left, right, (((left_dim,), (right_dim,)), ((), ())), pre...  170 us
    convert_element_type x1, other arithmetic, per_device(): jnp.stack([totals[0] for totals in totals_list]).astype(jnp.bfloat16)  91.3 us
    convert_element_type x1, other arithmetic, per_device(): jnp.stack([totals[2] for totals in totals_list]).astype(jnp.bfloat16)  46.8 us
    all_gather x1, waiting for transfers between devices, per_device(): lax.all_gather(signal_owned, 'ep', axis=0, tiled=True)  39.9 us
    all_gather x1, waiting for transfers between devices, per_device(): lax.all_gather(token_owned, 'ep', axis=0, tiled=True)  30.5 us
    all_to_all x1, blocking collectives, per_device(): lax.all_to_all(token_slots, 'group', split_axis=1, concat_axis=1, tiled=T...  10 us
    dot_general x1, matrix products, expert_signals(): up_pre = jnp.dot(token_rows, up_w, preferred_element_type=jnp.float32)  9.32 us
  transfers between devices with their start and end apart: 4, of which 2 were waited for; matrix products, arithmetic and copies ran while one was open for 43% of the time, Pallas kernels for 0%

commit v1 on v0

v1 whole, which is shorter than its diff:
```python
import functools

import jax
import jax.numpy as jnp
import numpy as np
from jax import lax
from jax.experimental import pallas as pl
from jax.experimental.pallas import tpu as pltpu
from jax.sharding import PartitionSpec as P

CAP = 5
COLD_CAP = 3

NT = (((1,), (1,)), ((), ()))
TN = (((0,), (0,)), ((), ()))
NN = (((1,), (0,)), ((), ()))


def mm(left, right, dims):
    return lax.dot_general(left, right, dims, preferred_element_type=jnp.float32)


def tile_of(inner, limit=344):
    fits = [t for t in range(8, limit + 1, 8) if inner % t == 0]
    return fits[-1] if fits else inner


def slot_map(route_block, prob_block, expert_index, capacity):
    named_hits = route_block[None, :, :] == expert_index[:, None, None]
    weight_sum = jnp.sum(jnp.where(named_hits, prob_block[None, :, :], 0.0), axis=2)
    chosen = jnp.any(named_hits, axis=2).astype(jnp.int32)
    position = jnp.cumsum(chosen, axis=1) - 1
    slot_index = jnp.arange(capacity, dtype=jnp.int32)
    onehot = (
        (position[:, None, :] == slot_index[None, :, None]) & (chosen[:, None, :] == 1)
    ).astype(jnp.float32)
    slot_weight = jnp.sum(onehot * weight_sum[:, None, :], axis=2)
    return (onehot, slot_weight)


def full(shape):
    return pl.BlockSpec(shape, lambda i: (0,) * len(shape), pipeline_mode=pl.Buffered(1))


def rows_of(tile, width):
    return pl.BlockSpec((tile, width), lambda i: (i, 0))


def masks_of(bits):
    masks = [0]
    for bit in bits:
        masks = masks + [m | (1 << bit) for m in masks]
    return masks


def split_kernel(order, block, chunk, perm_ref, a0_ref, a1_ref, b0_ref, b1_ref, t_ref, s_ref):
    perm = perm_ref[...]
    half = a0_ref.shape[1]
    pair = 2 * block
    per = a0_ref.shape[0] // pair
    count = 2 * per
    for side, refs in enumerate(((a0_ref, a1_ref), (b0_ref, b1_ref))):
        cols = slice(side * half, (side + 1) * half)
        for first in range(0, count, chunk):
            pieces = []
            for at in range(first, first + chunk):
                src = at if side == 0 else order[at]
                pieces.append(refs[src // per][(src % per) * pair : (src % per + 1) * pair, :])
            mixed = mm(perm, jnp.concatenate(pieces, axis=0), NN).astype(jnp.bfloat16)
            rows = slice(first * block, (first + chunk) * block)
            t_ref[rows, cols] = mixed[: chunk * block]
            s_ref[rows, cols] = mixed[chunk * block :]


def split_call(a0, a1, b0, b1, order, block):
    rows, half = a0.shape
    chunk = min(4, 2 * rows // (2 * block))
    size = 2 * block * chunk
    perm = np.zeros((size, size), np.float32)
    for side in range(2):
        for row in range(chunk * block):
            blk, rest = divmod(row, block)
            src, slot = divmod(rest, CAP)
            perm[side * chunk * block + row, blk * 2 * block + src * 2 * CAP + side * CAP + slot] = 1.0
    out = jax.ShapeDtypeStruct((rows, 2 * half), jnp.bfloat16)
    return pl.pallas_call(
        functools.partial(split_kernel, order, block, chunk),
        out_shape=[out, out],
        cost_estimate=pl.CostEstimate(flops=16 * rows * half * size // 4, bytes_accessed=16 * rows * half, transcendentals=0),
    )(jnp.asarray(perm, jnp.bfloat16), a0, a1, b0, b1)


def pre_kernel(t_ref, wg_ref, wu_ref, pg_ref, pu_ref):
    t = t_ref[...]
    pg_ref[...] = mm(wg_ref[...], t, NT)
    pu_ref[...] = mm(wu_ref[...], t, NT)


def pre_call(t, wg, wu):
    inner, width = wg.shape
    rows = t.shape[0]
    tile = tile_of(inner)
    return pl.pallas_call(
        pre_kernel,
        grid=(inner // tile,),
        in_specs=[full((rows, width)), rows_of(tile, width), rows_of(tile, width)],
        out_specs=[rows_of(tile, rows)] * 2,
        out_shape=[jax.ShapeDtypeStruct((inner, rows), jnp.float32)] * 2,
        cost_estimate=pl.CostEstimate(
            flops=4 * inner * width * rows, bytes_accessed=4 * inner * width, transcendentals=0
        ),
    )(t, wg, wu)


def signal_kernel(
    perm_ref, s_ref, wg_ref, wu_ref, wd_ref, pg_ref, pu_ref, h_ref, gs_ref, us_ref, dxa_ref, dxb_ref, acc_ref
):
    step = pl.program_id(0)
    gate = pg_ref[...]
    up = pu_ref[...]
    logistic = jax.nn.sigmoid(gate)
    swished = gate * logistic
    h_ref[...] = (swished * up).astype(jnp.bfloat16)
    hidden_grad = mm(wd_ref[...], s_ref[...], NT)
    gs = (hidden_grad * up * logistic * (1.0 + gate * (1.0 - logistic))).astype(jnp.bfloat16)
    us = (hidden_grad * swished).astype(jnp.bfloat16)
    gs_ref[...] = gs
    us_ref[...] = us
    part = mm(gs, wg_ref[...], TN) + mm(us, wu_ref[...], TN)

    @pl.when(step == 0)
    def _():
        acc_ref[...] = part

    @pl.when(step > 0)
    def _():
        acc_ref[...] += part

    @pl.when(step == pl.num_programs(0) - 1)
    def _():
        half = dxa_ref.shape[1]
        dxa_ref[...] = acc_ref[:, :half].astype(jnp.bfloat16)
        late = acc_ref[:, half:].astype(jnp.bfloat16)
        dxb_ref[...] = mm(perm_ref[...], late, NN).astype(jnp.bfloat16)


def signal_call(perm, s, wg, wu, wd, pg, pu):
    inner, width = wg.shape
    rows = s.shape[0]
    tile = tile_of(inner)
    return pl.pallas_call(
        signal_kernel,
        grid=(inner // tile,),
        in_specs=[full((rows, rows)), full((rows, width))] + [rows_of(tile, width)] * 3 + [rows_of(tile, rows)] * 2,
        out_specs=[rows_of(tile, rows)] * 3 + [full((rows, width // 2))] * 2,
        out_shape=[jax.ShapeDtypeStruct((inner, rows), jnp.bfloat16)] * 3
        + [jax.ShapeDtypeStruct((rows, width // 2), jnp.bfloat16)] * 2,
        scratch_shapes=[pltpu.VMEM((rows, width), jnp.float32)],
        cost_estimate=pl.CostEstimate(
            flops=6 * inner * width * rows, bytes_accessed=6 * inner * width, transcendentals=inner * rows
        ),
    )(perm, s, wg, wu, wd, pg, pu)


def weight_kernel(t_ref, s_ref, h_ref, gs_ref, us_ref, gg_ref, gu_ref, gd_ref):
    t = t_ref[...]
    gg_ref[...] = mm(gs_ref[...], t, NN).astype(jnp.bfloat16)
    gu_ref[...] = mm(us_ref[...], t, NN).astype(jnp.bfloat16)
    gd_ref[...] = mm(h_ref[...], s_ref[...], NN).astype(jnp.bfloat16)


def weight_call(t, s, h, gs, us):
    inner, rows = h.shape
    width = t.shape[1]
    tile = tile_of(inner)
    return pl.pallas_call(
        weight_kernel,
        grid=(inner // tile,),
        in_specs=[full((rows, width))] * 2 + [rows_of(tile, rows)] * 3,
        out_specs=[rows_of(tile, width)] * 3,
        out_shape=[jax.ShapeDtypeStruct((inner, width), jnp.bfloat16)] * 3,
        cost_estimate=pl.CostEstimate(
            flops=6 * inner * width * rows, bytes_accessed=6 * inner * width, transcendentals=0
        ),
    )(t, s, h, gs, us)


def swap(value, axis, size, offset):
    return lax.ppermute(value, axis, [(i, i ^ offset) for i in range(size)])


def per_device(tokens, out_grad, routes, gate_probs, hot, gate_weight, up_weight, down_weight):
    groups = lax.axis_size("group")
    slices = lax.axis_size("ep")
    width = tokens.shape[1]
    half = width // 2
    block = groups * CAP
    bits = slices.bit_length() - 1
    order_a = list(range(bits - 1, -1, -1))
    order_b = [0] + list(range(bits - 1, 0, -1))
    masks_a, masks_b = masks_of(order_a), masks_of(order_b)

    experts = jnp.arange(groups, dtype=jnp.int32) ^ lax.axis_index("group")
    onehot, slot_weight = slot_map(routes, gate_probs, experts, CAP)
    hot_id = jnp.remainder(hot[0], groups)
    slot_ids = jnp.arange(CAP, dtype=jnp.int32)
    retained = ((experts == hot_id)[:, None] | (slot_ids[None, :] < COLD_CAP)).astype(jnp.float32)
    pick = onehot * retained[:, :, None]
    weight = slot_weight * retained
    picker = pick.astype(jnp.bfloat16)
    token_slots = jnp.einsum("est,td->esd", picker, tokens, preferred_element_type=jnp.float32).astype(jnp.bfloat16)
    picked = jnp.einsum("est,td->esd", picker, out_grad, preferred_element_type=jnp.float32)
    signal_slots = (weight[:, :, None] * picked).astype(jnp.bfloat16)
    slots = jnp.concatenate([token_slots, signal_slots], axis=1)

    own = jnp.concatenate([slots[0]] + [swap(slots[k], "group", groups, k) for k in range(1, groups)], axis=0)

    held_a, held_b = own[:, :half], own[:, half:]
    for stage in range(bits):
        got_a = swap(held_a, "ep", slices, 1 << order_a[stage])
        got_b = swap(held_b, "ep", slices, 1 << order_b[stage])
        if stage < bits - 1:
            held_a = jnp.concatenate([held_a, got_a], axis=0)
            held_b = jnp.concatenate([held_b, got_b], axis=0)
    back = [masks_b.index(m) for m in masks_a]
    t, s = split_call(held_a, got_a, held_b, got_b, back, block)

    wg = jnp.swapaxes(gate_weight[0], 0, 1)
    wu = jnp.swapaxes(up_weight[0], 0, 1)
    wd = down_weight[0]
    pg, pu = pre_call(t, wg, wu)
    perm = np.zeros((slices * block,) * 2, np.float32)
    for at, mask in enumerate(masks_b):
        for row in range(block):
            perm[at * block + row, masks_a.index(mask) * block + row] = 1.0
    h, gs, us, dxa, dxb = signal_call(jnp.asarray(perm, jnp.bfloat16), s, wg, wu, wd, pg, pu)
    gg, gu, gd = weight_call(t, s, h, gs, us)

    for stage in range(bits - 1, -1, -1):
        sums = []
        for value, order in ((dxa, order_a), (dxb, order_b)):
            keep, send = value[: value.shape[0] // 2], value[value.shape[0] // 2 :]
            got = swap(send, "ep", slices, 1 << order[stage])
            sums.append((keep.astype(jnp.float32) + got.astype(jnp.float32)).astype(jnp.bfloat16))
        dxa, dxb = sums
    mine = jnp.concatenate([dxa, dxb], axis=1).reshape(groups, CAP, width)
    returned = jnp.stack([mine[0]] + [swap(mine[k], "group", groups, k) for k in range(1, groups)])
    tokens_grad = jnp.einsum("est,esd->td", picker, returned, preferred_element_type=jnp.float32).astype(jnp.bfloat16)
    return (tokens_grad, jnp.swapaxes(gg, 0, 1)[None], jnp.swapaxes(gu, 0, 1)[None], gd[None])


def solution(mesh):
    in_specs = (
        P(("group", "ep"), None),
        P(("group", "ep"), None),
        P(("group", "ep"), None),
        P(("group", "ep"), None),
        P(),
        P("group", None, "ep"),
        P("group", None, "ep"),
        P("group", "ep", None),
    )
    out_specs = (
        P(("group", "ep"), None),
        P("group", None, "ep"),
        P("group", None, "ep"),
        P("group", "ep", None),
    )
    return jax.shard_map(per_device, mesh=mesh, in_specs=in_specs, out_specs=out_specs, check_vma=False)
```

time: 459 us -> 144 us (0.31)
  matrix products: 192 us -> 2.16 us
  other arithmetic: 140 us -> 2.93 us
  Pallas kernels: 0 us -> 53.8 us
  starting transfers between devices: 3.53 us -> 25.4 us
  blocking collectives: 18.4 us -> 0 us
  waiting for transfers between devices: 70.4 us -> 54.2 us
  between operations: 15 us -> 1.73 us
  local copies, waits for them, and re-layouts: 16.1 us -> 3.07 us
    dot_general x18 -> x1, matrix products: 190 us -> 1.54 us  [per_device(): jnp.einsum('est,esd->td', picker, returned, preferred_element_type=jnp.fl...]
    convert_element_type x3 -> x7, other arithmetic: 138 us -> 0.36 us  [the longest x6 0.29 us: per_device(): (keep.astype(jnp.float32) + got.astype(jnp.float32)).astype(jnp.bfloat16)]
    all_gather x2 -> x0, waiting for transfers between devices: 70.4 us -> none  [the longest x1 39.9 us: per_device(): lax.all_gather(signal_owned, 'ep', axis=0, tiled=True)]
    ppermute x0 -> x18, waiting for transfers between devices: none -> 54.2 us  [swap(): return lax.ppermute(value, axis, [(i, i ^ offset) for i in range(size)])]
    pallas_call x0 -> x4, Pallas kernels: none -> 53.8 us  [the longest x1 23.6 us: signal_call(): pl.pallas_call(signal_kernel, grid=(inner // tile,), in_specs=[full((rows...]
    ppermute x0 -> x18, starting transfers between devices: none -> 25.4 us  [swap(): return lax.ppermute(value, axis, [(i, i ^ offset) for i in range(size)])]
    all_to_all x2 -> x0, blocking collectives: 18.4 us -> none  [the longest x1 10 us: per_device(): lax.all_to_all(token_slots, 'group', split_axis=1, concat_axis=1, tiled=T...]
    all_gather x4 -> x0, local copies, waits for them, and re-layouts: 7.01 us -> none  [the longest x2 4.18 us: per_device(): lax.all_gather(token_owned, 'ep', axis=0, tiled=True)]
  transfers between devices with their start and end apart: 4 -> 18, of which waited for: 2 -> 11; matrix products, arithmetic and copies ran while one was open for 43% -> 1% of each run, Pallas kernels for 0% -> 10%
where the time goes in v1:
time: 144 us; the launch traced here: 143 us
  waiting for transfers between devices  54.2 us (38%)
  Pallas kernels  53.8 us (37%)
  starting transfers between devices  25.4 us (18%)
  local copies, waits for them, and re-layouts  3.07 us (2%)
  other arithmetic  2.93 us (2%)
  matrix products  2.16 us (2%)
  between operations  1.73 us (1%)
    ppermute x18, waiting for transfers between devices, swap(): return lax.ppermute(value, axis, [(i, i ^ offset) for i in range(size)])  54.2 us
    ppermute x18, starting transfers between devices, swap(): return lax.ppermute(value, axis, [(i, i ^ offset) for i in range(size)])  25.4 us
    pallas_call x1, Pallas kernels, signal_call(): pl.pallas_call(signal_kernel, grid=(inner // tile,), in_specs=[full((rows...  23.6 us
    pallas_call x1, Pallas kernels, weight_call(): pl.pallas_call(weight_kernel, grid=(inner // tile,), in_specs=[full((rows...  14 us
    pallas_call x1, Pallas kernels, pre_call(): pl.pallas_call(pre_kernel, grid=(inner // tile,), in_specs=[full((rows, w...  12.2 us
    pallas_call x1, Pallas kernels, split_call(): pl.pallas_call(functools.partial(split_kernel, order, block, chunk), out_...  4.01 us
  transfers between devices with their start and end apart: 18, of which 11 were waited for; matrix products, arithmetic and copies ran while one was open for 1% of the time, Pallas kernels for 10%

profile of v1, /device:TPU:0, one launch (start us, length us, event | category | flops | bytes accessed | tf_op | source)
XLA Modules:
  0.0 143.2 jit_solution(3969913494376185053)
XLA Ops:
  5.0 2.6 %collective-permute-start.2 = (bf16[10,4096]{1,0:T(8,128)(2,1)S(1)}, bf16[10,4096]{1,0:T(8,128)(2,1)S(1)}, u32[]{:S(2)}, u32[]{:S(2)}) collective-permute-start(bf16[10,4096]{1,0:T(8,128)(2,1)S(1)} %get-tuple-element.30), channel_id=1, source_target_pairs={{0,24},{8,16},{16,8},{24,0},{1,25},{9,17},{17,9},{25,1},{2,26},{10... | collective-permute-start | bytes 245768 | tf_op jit(solution)/shard_map/ppermute | solution.py:189
  7.6 3.8 %collective-permute-done.2 = bf16[10,4096]{1,0:T(8,128)(2,1)S(1)} collective-permute-done((bf16[10,4096]{1,0:T(8,128)(2,1)S(1)}, bf16[10,4096]{1,0:T(8,128)(2,1)S(1)}, u32[]{:S(2)}, u32[]{:S(2)}) %collective-permute-start.2) | collective-permute-done | bytes 81952 | tf_op jit(solution)/shard_map/ppermute | solution.py:189
  11.5 3.0 %collective-permute-done.1 = bf16[10,4096]{1,0:T(8,128)(2,1)S(1)} collective-permute-done((bf16[10,4096]{1,0:T(8,128)(2,1)S(1)}, bf16[10,4096]{1,0:T(8,128)(2,1)S(1)}, u32[]{:S(2)}, u32[]{:S(2)}) %collective-permute-start.1) | collective-permute-done | bytes 81952 | tf_op jit(solution)/shard_map/ppermute | solution.py:189
  14.6 2.9 %collective-permute-start.3 = (bf16[40,2048]{1,0:T(8,128)(2,1)S(1)}, bf16[40,2048]{1,0:T(8,128)(2,1)S(1)}, u32[]{:S(2)}, u32[]{:S(2)}) collective-permute-start(bf16[40,2048]{1,0:T(8,128)(2,1)S(1)} %get-tuple-element.33), channel_id=1, source_target_pairs={{0,4},{1,5},{2,6},{3,7},{4,0},{5,1},{6,2},{7,3},{8,12},{9,13},{10,... | collective-permute-start | bytes 491528 | tf_op jit(solution)/shard_map/ppermute | solution.py:189
  19.0 6.0 %collective-permute-done.3 = bf16[40,2048]{1,0:T(8,128)(2,1)S(1)} collective-permute-done((bf16[40,2048]{1,0:T(8,128)(2,1)S(1)}, bf16[40,2048]{1,0:T(8,128)(2,1)S(1)}, u32[]{:S(2)}, u32[]{:S(2)}) %collective-permute-start.3) | collective-permute-done | bytes 163872 | tf_op jit(solution)/shard_map/ppermute | solution.py:189
  25.7 3.4 %collective-permute-start.7 = (bf16[80,2048]{1,0:T(8,128)(2,1)S(1)}, bf16[80,2048]{1,0:T(8,128)(2,1)S(1)}, u32[]{:S(2)}, u32[]{:S(2)}) collective-permute-start(bf16[80,2048]{1,0:T(8,128)(2,1)S(1)} %pad_maximum_fusion.4), channel_id=1, source_target_pairs={{0,4},{1,5},{2,6},{3,7},{4,0},{5,1},{6,2},{7,3},{8,12},{9,13},{10,... | collective-permute-start | bytes 983048 | tf_op jit(solution)/shard_map/ppermute | solution.py:189
  29.2 11.4 %collective-permute-done.4 = bf16[80,2048]{1,0:T(8,128)(2,1)S(1)} collective-permute-done((bf16[80,2048]{1,0:T(8,128)(2,1)S(1)}, bf16[80,2048]{1,0:T(8,128)(2,1)S(1)}, u32[]{:S(2)}, u32[]{:S(2)}) %collective-permute-start.4) | collective-permute-done | bytes 327712 | tf_op jit(solution)/shard_map/ppermute | solution.py:189
  42.0 1.9 %collective-permute-done.7 = bf16[80,2048]{1,0:T(8,128)(2,1)S(1)} collective-permute-done((bf16[80,2048]{1,0:T(8,128)(2,1)S(1)}, bf16[80,2048]{1,0:T(8,128)(2,1)S(1)}, u32[]{:S(2)}, u32[]{:S(2)}) %collective-permute-start.7) | collective-permute-done | bytes 327712 | tf_op jit(solution)/shard_map/ppermute | solution.py:189
  44.2 11.4 %collective-permute-done.5.a1_ref = bf16[160,2048]{1,0:T(8,128)(2,1)S(1)} collective-permute-done((bf16[160,2048]{1,0:T(8,128)(2,1)S(1)}, bf16[160,2048]{1,0:T(8,128)(2,1)S(1)}, u32[]{:S(2)}, u32[]{:S(2)}) %collective-permute-start.5) | collective-permute-done | bytes 655392 | tf_op jit(solution)/shard_map/ppermute | solution.py:189
  55.7 2.8 %collective-permute-done.8.b1_ref = bf16[160,2048]{1,0:T(8,128)(2,1)S(1)} collective-permute-done((bf16[160,2048]{1,0:T(8,128)(2,1)S(1)}, bf16[160,2048]{1,0:T(8,128)(2,1)S(1)}, u32[]{:S(2)}, u32[]{:S(2)}) %collective-permute-start.8) | collective-permute-done | bytes 655392 | tf_op jit(solution)/shard_map/ppermute | solution.py:189
  59.4 4.0 %shard_map.129 = (bf16[160,4096]{1,0:T(8,128)(2,1)}, bf16[160,4096]{1,0:T(8,128)(2,1)}) custom-call(bf16[160,160]{1,0:T(8,128)(2,1)} %constant.38.clone.perm_ref, bf16[160,2048]{1,0:T(8,128)(2,1)} %copy-done.2, bf16[160,2048]{1,0:T(8,128)(2,1)} %copy-done.7, bf16[160,2048]{1,0:T(8,128)(2,1)} %copy-done.3, bf16[160,2048]{1,0:T(8,128)(2,1)} %copy-done.8), custom_call_target="tpu_custom_call" | custom-call | flops 209715200 | bytes 5242880 | tf_op jit(solution)/shard_map/pallas_call | solution.py:86
  63.4 12.2 %shard_map.130 = (f32[1376,160]{1,0:T(8,128)}, f32[1376,160]{1,0:T(8,128)}) custom-call(bf16[160,4096]{1,0:T(8,128)(2,1)} %get-tuple-element.17.t_ref, bf16[1376,4096]{1,0:T(8,128)(2,1)} %bitcast.41, bf16[1376,4096]{1,0:T(8,128)(2,1)} %bitcast.43), custom_call_target="tpu_custom_call" | custom-call | flops 3607101440 | bytes 22544384 | tf_op jit(solution)/shard_map/pallas_call | solution.py:103
  75.6 23.6 %shard_map.131 = (bf16[1376,160]{1,0:T(8,128)(2,1)}, bf16[1376,160]{1,0:T(8,128)(2,1)}, bf16[1376,160]{1,0:T(8,128)(2,1)}, bf16[160,2048]{1,0:T(8,128)(2,1)}, bf16[160,2048]{1,0:T(8,128)(2,1)}) custom-call(bf16[160,160]{1,0:T(8,128)(2,1)} %constant.39.clone.perm_ref, bf16[160,4096]{1,0:T(8,128)(2,1)} %get-tuple-element.16.s_ref, ...), custom_call_target="tpu_custom_call" | custom-call | flops 5410652160 | bytes 33816576 | tf_op jit(solution)/shard_map/pallas_call | solution.py:151
  100.3 1.8 %collective-permute-start.12 = (bf16[80,2048]{1,0:T(8,128)(2,1)S(1)}, bf16[80,2048]{1,0:T(8,128)(2,1)S(1)}, u32[]{:S(2)}, u32[]{:S(2)}) collective-permute-start(bf16[80,2048]{1,0:T(8,128)(2,1)S(1)} %slice.85), channel_id=1, source_target_pairs={{0,2},{1,3},{2,0},{3,1},{4,6},{5,7},{6,4},{7,5},{8,10},{9,11},{10,... | collective-permute-start | bytes 983048 | tf_op jit(solution)/shard_map/ppermute | solution.py:189
  103.1 1.6 %collective-permute-start.9 = (bf16[80,2048]{1,0:T(8,128)(2,1)S(1)}, bf16[80,2048]{1,0:T(8,128)(2,1)S(1)}, u32[]{:S(2)}, u32[]{:S(2)}) collective-permute-start(bf16[80,2048]{1,0:T(8,128)(2,1)S(1)} %slice.79), channel_id=1, source_target_pairs={{0,1},{1,0},{2,3},{3,2},{4,5},{5,4},{6,7},{7,6},{8,9},{9,8},{10,11... | collective-permute-start | bytes 983048 | tf_op jit(solution)/shard_map/ppermute | solution.py:189
  104.7 3.8 %collective-permute-done.12 = bf16[80,2048]{1,0:T(8,128)(2,1)S(1)} collective-permute-done((bf16[80,2048]{1,0:T(8,128)(2,1)S(1)}, bf16[80,2048]{1,0:T(8,128)(2,1)S(1)}, u32[]{:S(2)}, u32[]{:S(2)}) %collective-permute-start.12) | collective-permute-done | bytes 327712 | tf_op jit(solution)/shard_map/ppermute | solution.py:189
  108.6 2.6 %collective-permute-start.13 = (bf16[40,2048]{1,0:T(8,128)(2,1)S(1)}, bf16[40,2048]{1,0:T(8,128)(2,1)S(1)}, u32[]{:S(2)}, u32[]{:S(2)}) collective-permute-start(bf16[40,2048]{1,0:T(8,128)(2,1)S(1)} %slice.108), channel_id=1, source_target_pairs={{0,4},{1,5},{2,6},{3,7},{4,0},{5,1},{6,2},{7,3},{8,12},{9,13},{10,... | collective-permute-start | bytes 491528 | tf_op jit(solution)/shard_map/ppermute | solution.py:189
  112.8 4.2 %collective-permute-done.13 = bf16[40,2048]{1,0:T(8,128)(2,1)S(1)} collective-permute-done((bf16[40,2048]{1,0:T(8,128)(2,1)S(1)}, bf16[40,2048]{1,0:T(8,128)(2,1)S(1)}, u32[]{:S(2)}, u32[]{:S(2)}) %collective-permute-start.13) | collective-permute-done | bytes 163872 | tf_op jit(solution)/shard_map/ppermute | solution.py:189
  117.1 1.6 %collective-permute-start.14 = (bf16[20,2048]{1,0:T(8,128)(2,1)S(1)}, bf16[20,2048]{1,0:T(8,128)(2,1)S(1)}, u32[]{:S(2)}, u32[]{:S(2)}) collective-permute-start(bf16[20,2048]{1,0:T(8,128)(2,1)S(1)} %slice.110), channel_id=1, source_target_pairs={{0,1},{1,0},{2,3},{3,2},{4,5},{5,4},{6,7},{7,6},{8,9},{9,8},{10,11... | collective-permute-start | bytes 245768 | tf_op jit(solution)/shard_map/ppermute | solution.py:189
  119.6 2.1 %collective-permute-done.14 = bf16[20,2048]{1,0:T(8,128)(2,1)S(1)} collective-permute-done((bf16[20,2048]{1,0:T(8,128)(2,1)S(1)}, bf16[20,2048]{1,0:T(8,128)(2,1)S(1)}, u32[]{:S(2)}, u32[]{:S(2)}) %collective-permute-start.14) | collective-permute-done | bytes 81952 | tf_op jit(solution)/shard_map/ppermute | solution.py:189
  121.8 3.6 %collective-permute-done.11 = bf16[20,2048]{1,0:T(8,128)(2,1)S(1)} collective-permute-done((bf16[20,2048]{1,0:T(8,128)(2,1)S(1)}, bf16[20,2048]{1,0:T(8,128)(2,1)S(1)}, u32[]{:S(2)}, u32[]{:S(2)}) %collective-permute-start.11) | collective-permute-done | bytes 81952 | tf_op jit(solution)/shard_map/ppermute | solution.py:189
  125.5 1.6 %collective-permute-start.17 = (bf16[5,4096]{1,0:T(8,128)(2,1)S(1)}, bf16[5,4096]{1,0:T(8,128)(2,1)S(1)}, u32[]{:S(2)}, u32[]{:S(2)}) collective-permute-start(bf16[5,4096]{1,0:T(8,128)(2,1)S(1)} %get-tuple-element.36), channel_id=1, source_target_pairs={{0,24},{8,16},{16,8},{24,0},{1,25},{9,17},{17,9},{25,1},{2,26},{10... | collective-permute-start | bytes 122888 | tf_op jit(solution)/shard_map/ppermute | solution.py:189
  127.7 14.0 %shard_map.132 = (bf16[1376,4096]{1,0:T(8,128)(2,1)}, bf16[1376,4096]{1,0:T(8,128)(2,1)}, bf16[1376,4096]{1,0:T(8,128)(2,1)}) custom-call(bf16[160,4096]{1,0:T(8,128)(2,1)} %get-tuple-element.17.t_ref, bf16[160,4096]{1,0:T(8,128)(2,1)} %get-tuple-element.16.s_ref, bf16[1376,160]{1,0:T(8,128)(2,1)} %get-tuple-element.22.h_ref, ...), custom_call_target="tpu_custom_call" | custom-call | flops 5410652160 | bytes 33816576 | tf_op jit(solution)/shard_map/pallas_call | solution.py:176
  141.7 1.5 %fusion = bf16[128,4096]{1,0:T(8,128)(2,1)} fusion(bf16[1,5,4096]{2,1,0:T(8,128)(2,1)S(1)} %bitcast.47, bf16[1,5,4096]{2,1,0:T(8,128)(2,1)S(1)} %bitcast.48, bf16[1,5,4096]{2,1,0:T(8,128)(2,1)S(1)} %bitcast.46, bf16[1,5,4096]{2,1,0:T(8,128)(2,1)S(1)} %get-tuple-element.34, bf16[4,5]{1,0:T(4,128)(2,1)S(1)} %or_convert_fusion, ...), kind=kOutput, calls=%fused_computation.1 | convolution fusion | flops 21749248 | bytes 1215016 | tf_op jit(solution)/shard_map/est,esd->td/dot_general | solution.py:248
  (68 shorter events, 14.0 us)
Async XLA Ops:
  0.6 3.0 %copy-start = (bf16[128,4096]{1,0:T(8,128)(2,1)S(1)}, bf16[128,4096]{1,0:T(8,128)(2,1)}, u32[]{:S(2)}) copy-start(bf16[128,4096]{1,0:T(8,128)(2,1)} %param.10) | copy-start | bytes 3145732
  0.6 3.3 %copy-start.4 = (bf16[128,4096]{1,0:T(8,128)(2,1)S(1)}, bf16[128,4096]{1,0:T(8,128)(2,1)}, u32[]{:S(2)}) copy-start(bf16[128,4096]{1,0:T(8,128)(2,1)} %param.11) | copy-start | bytes 3145732
  4.4 3.2 %collective-permute-start = (bf16[10,4096]{1,0:T(8,128)(2,1)S(1)}, bf16[10,4096]{1,0:T(8,128)(2,1)S(1)}, u32[]{:S(2)}, u32[]{:S(2)}) collective-permute-start(bf16[10,4096]{1,0:T(8,128)(2,1)S(1)} %get-tuple-element.29), channel_id=1, source_target_pairs={{0,8},{8,0},{16,24},{24,16},{1,9},{9,1},{17,25},{25,17},{2,10},{10... | collective-permute-start | bytes 245768 | tf_op jit(solution)/shard_map/ppermute | solution.py:189
  5.0 6.5 %collective-permute-start.2 = (bf16[10,4096]{1,0:T(8,128)(2,1)S(1)}, bf16[10,4096]{1,0:T(8,128)(2,1)S(1)}, u32[]{:S(2)}, u32[]{:S(2)}) collective-permute-start(bf16[10,4096]{1,0:T(8,128)(2,1)S(1)} %get-tuple-element.30), channel_id=1, source_target_pairs={{0,24},{8,16},{16,8},{24,0},{1,25},{9,17},{17,9},{25,1},{2,26},{10... | collective-permute-start | bytes 245768 | tf_op jit(solution)/shard_map/ppermute | solution.py:189
  7.6 6.9 %collective-permute-start.1 = (bf16[10,4096]{1,0:T(8,128)(2,1)S(1)}, bf16[10,4096]{1,0:T(8,128)(2,1)S(1)}, u32[]{:S(2)}, u32[]{:S(2)}) collective-permute-start(bf16[10,4096]{1,0:T(8,128)(2,1)S(1)} %get-tuple-element.31), channel_id=1, source_target_pairs={{0,16},{8,24},{16,0},{24,8},{1,17},{9,25},{17,1},{25,9},{2,18},{10... | collective-permute-start | bytes 245768 | tf_op jit(solution)/shard_map/ppermute | solution.py:189
  14.6 10.4 %collective-permute-start.3 = (bf16[40,2048]{1,0:T(8,128)(2,1)S(1)}, bf16[40,2048]{1,0:T(8,128)(2,1)S(1)}, u32[]{:S(2)}, u32[]{:S(2)}) collective-permute-start(bf16[40,2048]{1,0:T(8,128)(2,1)S(1)} %get-tuple-element.33), channel_id=1, source_target_pairs={{0,4},{1,5},{2,6},{3,7},{4,0},{5,1},{6,2},{7,3},{8,12},{9,13},{10,... | collective-permute-start | bytes 491528 | tf_op jit(solution)/shard_map/ppermute | solution.py:189
  17.5 8.2 %collective-permute-start.6 = (bf16[40,2048]{1,0:T(8,128)(2,1)S(1)}, bf16[40,2048]{1,0:T(8,128)(2,1)S(1)}, u32[]{:S(2)}, u32[]{:S(2)}) collective-permute-start(bf16[40,2048]{1,0:T(8,128)(2,1)S(1)} %get-tuple-element.32), channel_id=1, source_target_pairs={{0,1},{1,0},{2,3},{3,2},{4,5},{5,4},{6,7},{7,6},{8,9},{9,8},{10,11... | collective-permute-start | bytes 491528 | tf_op jit(solution)/shard_map/ppermute | solution.py:189
  25.1 15.5 %collective-permute-start.4 = (bf16[80,2048]{1,0:T(8,128)(2,1)S(1)}, bf16[80,2048]{1,0:T(8,128)(2,1)S(1)}, u32[]{:S(2)}, u32[]{:S(2)}) collective-permute-start(bf16[80,2048]{1,0:T(8,128)(2,1)S(1)} %pad_maximum_fusion.3), channel_id=1, source_target_pairs={{0,2},{1,3},{2,0},{3,1},{4,6},{5,7},{6,4},{7,5},{8,10},{9,11},{10,... | collective-permute-start | bytes 983048 | tf_op jit(solution)/shard_map/ppermute | solution.py:189
  25.7 18.1 %collective-permute-start.7 = (bf16[80,2048]{1,0:T(8,128)(2,1)S(1)}, bf16[80,2048]{1,0:T(8,128)(2,1)S(1)}, u32[]{:S(2)}, u32[]{:S(2)}) collective-permute-start(bf16[80,2048]{1,0:T(8,128)(2,1)S(1)} %pad_maximum_fusion.4), channel_id=1, source_target_pairs={{0,4},{1,5},{2,6},{3,7},{4,0},{5,1},{6,2},{7,3},{8,12},{9,13},{10,... | collective-permute-start | bytes 983048 | tf_op jit(solution)/shard_map/ppermute | solution.py:189
  40.7 17.8 %copy-start.2 = (bf16[160,2048]{1,0:T(8,128)(2,1)}, bf16[160,2048]{1,0:T(8,128)(2,1)S(1)}, u32[]{:S(2)}) copy-start(bf16[160,2048]{1,0:T(8,128)(2,1)S(1)} %pad_maximum_fusion.a0_ref) | copy-start | bytes 1966084
  40.7 15.0 %collective-permute-start.5 = (bf16[160,2048]{1,0:T(8,128)(2,1)S(1)}, bf16[160,2048]{1,0:T(8,128)(2,1)S(1)}, u32[]{:S(2)}, u32[]{:S(2)}) collective-permute-start(bf16[160,2048]{1,0:T(8,128)(2,1)S(1)} %pad_maximum_fusion.a0_ref), channel_id=1, source_target_pairs={{0,1},{1,0},{2,3},{3,2},{4,5},{5,4},{6,7},{7,6},{8,9},{9,8},{10,11... | collective-permute-start | bytes 1966088 | tf_op jit(solution)/shard_map/ppermute | solution.py:189
  43.9 14.6 %copy-start.3 = (bf16[160,2048]{1,0:T(8,128)(2,1)}, bf16[160,2048]{1,0:T(8,128)(2,1)S(1)}, u32[]{:S(2)}) copy-start(bf16[160,2048]{1,0:T(8,128)(2,1)S(1)} %pad_maximum_fusion.1.b0_ref) | copy-start | bytes 1966084
  43.9 14.6 %collective-permute-start.8 = (bf16[160,2048]{1,0:T(8,128)(2,1)S(1)}, bf16[160,2048]{1,0:T(8,128)(2,1)S(1)}, u32[]{:S(2)}, u32[]{:S(2)}) collective-permute-start(bf16[160,2048]{1,0:T(8,128)(2,1)S(1)} %pad_maximum_fusion.1.b0_ref), channel_id=1, source_target_pairs={{0,2},{1,3},{2,0},{3,1},{4,6},{5,7},{6,4},{7,5},{8,10},{9,11},{10,... | collective-permute-start | bytes 1966088 | tf_op jit(solution)/shard_map/ppermute | solution.py:189
  99.2 9.3 %copy-start.6 = (bf16[160,2048]{1,0:T(8,128)(2,1)S(1)}, bf16[160,2048]{1,0:T(8,128)(2,1)}, u32[]{:S(2)}) copy-start(bf16[160,2048]{1,0:T(8,128)(2,1)} %get-tuple-element.21) | copy-start | bytes 1966084
  99.2 12.0 %copy-start.5 = (bf16[160,2048]{1,0:T(8,128)(2,1)S(1)}, bf16[160,2048]{1,0:T(8,128)(2,1)}, u32[]{:S(2)}) copy-start(bf16[160,2048]{1,0:T(8,128)(2,1)} %get-tuple-element.20) | copy-start | bytes 1966084
  100.3 8.2 %collective-permute-start.12 = (bf16[80,2048]{1,0:T(8,128)(2,1)S(1)}, bf16[80,2048]{1,0:T(8,128)(2,1)S(1)}, u32[]{:S(2)}, u32[]{:S(2)}) collective-permute-start(bf16[80,2048]{1,0:T(8,128)(2,1)S(1)} %slice.85), channel_id=1, source_target_pairs={{0,2},{1,3},{2,0},{3,1},{4,6},{5,7},{6,4},{7,5},{8,10},{9,11},{10,... | collective-permute-start | bytes 983048 | tf_op jit(solution)/shard_map/ppermute | solution.py:189
  103.1 8.1 %collective-permute-start.9 = (bf16[80,2048]{1,0:T(8,128)(2,1)S(1)}, bf16[80,2048]{1,0:T(8,128)(2,1)S(1)}, u32[]{:S(2)}, u32[]{:S(2)}) collective-permute-start(bf16[80,2048]{1,0:T(8,128)(2,1)S(1)} %slice.79), channel_id=1, source_target_pairs={{0,1},{1,0},{2,3},{3,2},{4,5},{5,4},{6,7},{7,6},{8,9},{9,8},{10,11... | collective-permute-start | bytes 983048 | tf_op jit(solution)/shard_map/ppermute | solution.py:189
  108.6 8.4 %collective-permute-start.13 = (bf16[40,2048]{1,0:T(8,128)(2,1)S(1)}, bf16[40,2048]{1,0:T(8,128)(2,1)S(1)}, u32[]{:S(2)}, u32[]{:S(2)}) collective-permute-start(bf16[40,2048]{1,0:T(8,128)(2,1)S(1)} %slice.108), channel_id=1, source_target_pairs={{0,4},{1,5},{2,6},{3,7},{4,0},{5,1},{6,2},{7,3},{8,12},{9,13},{10,... | collective-permute-start | bytes 491528 | tf_op jit(solution)/shard_map/ppermute | solution.py:189
  111.3 7.3 %collective-permute-start.10 = (bf16[40,2048]{1,0:T(8,128)(2,1)S(1)}, bf16[40,2048]{1,0:T(8,128)(2,1)S(1)}, u32[]{:S(2)}, u32[]{:S(2)}) collective-permute-start(bf16[40,2048]{1,0:T(8,128)(2,1)S(1)} %slice.104), channel_id=1, source_target_pairs={{0,2},{1,3},{2,0},{3,1},{4,6},{5,7},{6,4},{7,5},{8,10},{9,11},{10,... | collective-permute-start | bytes 491528 | tf_op jit(solution)/shard_map/ppermute | solution.py:189
  117.1 4.7 %collective-permute-start.14 = (bf16[20,2048]{1,0:T(8,128)(2,1)S(1)}, bf16[20,2048]{1,0:T(8,128)(2,1)S(1)}, u32[]{:S(2)}, u32[]{:S(2)}) collective-permute-start(bf16[20,2048]{1,0:T(8,128)(2,1)S(1)} %slice.110), channel_id=1, source_target_pairs={{0,1},{1,0},{2,3},{3,2},{4,5},{5,4},{6,7},{7,6},{8,9},{9,8},{10,11... | collective-permute-start | bytes 245768 | tf_op jit(solution)/shard_map/ppermute | solution.py:189
  118.7 6.6 %collective-permute-start.11 = (bf16[20,2048]{1,0:T(8,128)(2,1)S(1)}, bf16[20,2048]{1,0:T(8,128)(2,1)S(1)}, u32[]{:S(2)}, u32[]{:S(2)}) collective-permute-start(bf16[20,2048]{1,0:T(8,128)(2,1)S(1)} %slice.106), channel_id=1, source_target_pairs={{0,4},{1,5},{2,6},{3,7},{4,0},{5,1},{6,2},{7,3},{8,12},{9,13},{10,... | collective-permute-start | bytes 245768 | tf_op jit(solution)/shard_map/ppermute | solution.py:189
  125.5 16.2 %collective-permute-start.15 = (bf16[5,4096]{1,0:T(8,128)(2,1)S(1)}, bf16[5,4096]{1,0:T(8,128)(2,1)S(1)}, u32[]{:S(2)}, u32[]{:S(2)}) collective-permute-start(bf16[5,4096]{1,0:T(8,128)(2,1)S(1)} %get-tuple-element.35), channel_id=1, source_target_pairs={{0,8},{8,0},{16,24},{24,16},{1,9},{9,1},{17,25},{25,17},{2,10},{10... | collective-permute-start | bytes 122888 | tf_op jit(solution)/shard_map/ppermute | solution.py:189
  125.5 16.1 %collective-permute-start.17 = (bf16[5,4096]{1,0:T(8,128)(2,1)S(1)}, bf16[5,4096]{1,0:T(8,128)(2,1)S(1)}, u32[]{:S(2)}, u32[]{:S(2)}) collective-permute-start(bf16[5,4096]{1,0:T(8,128)(2,1)S(1)} %get-tuple-element.36), channel_id=1, source_target_pairs={{0,24},{8,16},{16,8},{24,0},{1,25},{9,17},{17,9},{25,1},{2,26},{10... | collective-permute-start | bytes 122888 | tf_op jit(solution)/shard_map/ppermute | solution.py:189
  127.1 14.5 %collective-permute-start.16 = (bf16[5,4096]{1,0:T(8,128)(2,1)S(1)}, bf16[5,4096]{1,0:T(8,128)(2,1)S(1)}, u32[]{:S(2)}, u32[]{:S(2)}) collective-permute-start(bf16[5,4096]{1,0:T(8,128)(2,1)S(1)} %get-tuple-element.37), channel_id=1, source_target_pairs={{0,16},{8,24},{16,0},{24,8},{1,17},{9,25},{17,1},{25,9},{2,18},{10... | collective-permute-start | bytes 122888 | tf_op jit(solution)/shard_map/ppermute | solution.py:189
  (3 other events, 5.2 us)

commit v2 on v1

v2 whole, which is shorter than its diff:
```python
import functools

import jax
import jax.numpy as jnp
import numpy as np
from jax import lax
from jax.experimental import pallas as pl
from jax.experimental.pallas import tpu as pltpu
from jax.sharding import PartitionSpec as P

CAP = 5
COLD_CAP = 3
SLOTS = 3
STEP = 512
BANDS = 4
SMALL_MIB = 12
SPARE_MIB = 16

NT = (((1,), (1,)), ((), ()))
TN = (((0,), (0,)), ((), ()))
NN = (((1,), (0,)), ((), ()))


def mm(left, right, dims):
    return lax.dot_general(left, right, dims, preferred_element_type=jnp.float32)


def tile_of(inner, limit=344):
    fits = [t for t in range(8, limit + 1, 8) if inner % t == 0]
    return fits[-1] if fits else inner


def slot_map(route_block, prob_block, expert_index, capacity):
    named_hits = route_block[None, :, :] == expert_index[:, None, None]
    weight_sum = jnp.sum(jnp.where(named_hits, prob_block[None, :, :], 0.0), axis=2)
    chosen = jnp.any(named_hits, axis=2).astype(jnp.int32)
    position = jnp.cumsum(chosen, axis=1) - 1
    slot_index = jnp.arange(capacity, dtype=jnp.int32)
    onehot = (
        (position[:, None, :] == slot_index[None, :, None]) & (chosen[:, None, :] == 1)
    ).astype(jnp.float32)
    slot_weight = jnp.sum(onehot * weight_sum[:, None, :], axis=2)
    return (onehot, slot_weight)


def full(shape):
    return pl.BlockSpec(shape, lambda i: (0,) * len(shape), pipeline_mode=pl.Buffered(1))


def rows_of(tile, width):
    return pl.BlockSpec((tile, width), lambda i: (i, 0))


def masks_of(bits):
    masks = [0]
    for bit in bits:
        masks = masks + [m | (1 << bit) for m in masks]
    return masks


def join(perm, refs):
    a0, a1, b0, b1 = (ref[...] for ref in refs)
    late = mm(perm, jnp.concatenate([b0, b1], axis=0), NN).astype(jnp.bfloat16)
    return jnp.concatenate([jnp.concatenate([a0, a1], axis=0), late], axis=1)


def cuts_of(inner, step):
    return [(low, min(low + step, inner)) for low in range(0, inner, step)]


VMEM = pl.BlockSpec(memory_space=pltpu.VMEM)
ANY = pl.BlockSpec(memory_space=pl.ANY)


def load_kernel(cuts, w_hbm, w_ref, sems):
    copies = []
    for at, (low, high) in enumerate(cuts):
        rows = pl.ds(low, high - low)
        copies.append(pltpu.make_async_copy(w_hbm.at[rows, :], w_ref.at[rows, :], sems.at[at]))
        copies[at].start()
    for copy in copies:
        copy.wait()


def load_call(w, before):
    size = 2 * w.size
    grant = (63 << 20) - (before + 1) * size - min(6 << 20, size // 2)
    cuts = cuts_of(w.shape[0], 344)
    return pl.pallas_call(
        functools.partial(load_kernel, cuts),
        in_specs=[pl.BlockSpec(memory_space=pltpu.HBM)],
        out_specs=VMEM,
        out_shape=pltpu.VMEM(w.shape, w.dtype),
        scratch_shapes=[pltpu.SemaphoreType.DMA((len(cuts),))],
        compiler_params=pltpu.CompilerParams(vmem_limit_bytes=grant),
        cost_estimate=pl.CostEstimate(flops=0, bytes_accessed=2 * w.size, transcendentals=0),
    )(w)


def gate_kernel(cuts, perm_ref, a0_ref, a1_ref, b0_ref, b1_ref, wg_ref, t_ref, pg_ref):
    t = join(perm_ref[...], (a0_ref, a1_ref, b0_ref, b1_ref))
    t_ref[...] = t
    for low, high in cuts:
        pg_ref[low:high, :] = mm(wg_ref[low:high, :], t, NT)


def gate_call(perm, parts, wg):
    inner, width = wg.shape
    rows = perm.shape[0]
    return pl.pallas_call(
        functools.partial(gate_kernel, cuts_of(inner, STEP)),
        in_specs=[VMEM] * 6,
        out_specs=[VMEM] * 2,
        out_shape=[
            jax.ShapeDtypeStruct((rows, width), jnp.bfloat16),
            jax.ShapeDtypeStruct((inner, rows), jnp.float32),
        ],
        compiler_params=pltpu.CompilerParams(vmem_limit_bytes=SMALL_MIB << 20),
        cost_estimate=pl.CostEstimate(
            flops=2 * inner * width * rows, bytes_accessed=2 * inner * width, transcendentals=0
        ),
    )(perm, *parts, wg)


def up_kernel(cuts, t_ref, wu_ref, pu_ref):
    t = t_ref[...]
    for low, high in cuts:
        pu_ref[low:high, :] = mm(wu_ref[low:high, :], t, NT)


def up_call(t, wu):
    inner, width = wu.shape
    rows = t.shape[0]
    return pl.pallas_call(
        functools.partial(up_kernel, cuts_of(inner, STEP)),
        in_specs=[VMEM] * 2,
        out_specs=VMEM,
        out_shape=jax.ShapeDtypeStruct((inner, rows), jnp.float32),
        compiler_params=pltpu.CompilerParams(vmem_limit_bytes=SMALL_MIB << 20),
        cost_estimate=pl.CostEstimate(
            flops=2 * inner * width * rows, bytes_accessed=2 * inner * width, transcendentals=0
        ),
    )(t, wu)


def signal_kernel(
    cuts, perm_ref, back_ref, a0_ref, a1_ref, b0_ref, b1_ref, pg_ref, pu_ref, wg_ref, wu_hbm, wd_hbm,
    s_ref, h_ref, gs_ref, us_ref, keepa_ref, senda_ref, keepb_ref, sendb_ref, acc_ref, wu_ref, wd_ref, sems,
):
    copies = []
    for side, (src, dst) in enumerate(((wd_hbm, wd_ref), (wu_hbm, wu_ref))):
        for at, (low, high) in enumerate(cuts):
            rows = pl.ds(low, high - low)
            copies.append(pltpu.make_async_copy(src.at[rows, :], dst.at[rows, :], sems.at[side, at]))
    for copy in copies[: len(cuts)]:
        copy.start()
    s = join(perm_ref[...], (a0_ref, a1_ref, b0_ref, b1_ref))
    s_ref[...] = s
    for at, (low, high) in enumerate(cuts):
        gate = pg_ref[low:high, :]
        up = pu_ref[low:high, :]
        logistic = jax.nn.sigmoid(gate)
        swished = gate * logistic
        h_ref[low:high, :] = (swished * up).astype(jnp.bfloat16)
        copies[at].wait()
        copies[len(cuts) + at].start()
        hidden_grad = mm(wd_ref[low:high, :], s, NT)
        gs_ref[low:high, :] = (hidden_grad * up * logistic * (1.0 + gate * (1.0 - logistic))).astype(jnp.bfloat16)
        us_ref[low:high, :] = (hidden_grad * swished).astype(jnp.bfloat16)
    half = keepa_ref.shape[1]
    kept = keepa_ref.shape[0]
    wide = 2 * half // BANDS
    bands = [slice(band * wide, (band + 1) * wide) for band in range(BANDS)]
    gs = gs_ref[...].T
    for cols in bands:
        acc_ref[:, cols] = mm(gs, wg_ref[:, cols], NN)
    us = us_ref[...].T
    for copy in copies[len(cuts) :]:
        copy.wait()
    for cols in bands:
        part = (acc_ref[:, cols] + mm(us, wu_ref[:, cols], NN)).astype(jnp.bfloat16)
        if cols.start < half:
            keepa_ref[:, cols] = part[:kept]
            senda_ref[:, cols] = part[kept:]
        else:
            there = slice(cols.start - half, cols.stop - half)
            late = mm(back_ref[...], part, NN).astype(jnp.bfloat16)
            keepb_ref[:, there] = late[:kept]
            sendb_ref[:, there] = late[kept:]


def signal_call(perm, back, parts, pg, pu, wg, wu, wd):
    inner, width = wg.shape
    rows = perm.shape[0]
    cuts = cuts_of(inner, 256)
    grant = (63 << 20) - 2 * wg.size - (SPARE_MIB << 20)
    return pl.pallas_call(
        functools.partial(signal_kernel, cuts),
        in_specs=[VMEM] * 9 + [ANY] * 2,
        out_specs=[VMEM] * 8,
        out_shape=[jax.ShapeDtypeStruct((rows, width), jnp.bfloat16)]
        + [jax.ShapeDtypeStruct((inner, rows), jnp.bfloat16)] * 3
        + [jax.ShapeDtypeStruct((rows // 2, width // 2), jnp.bfloat16)] * 4,
        scratch_shapes=[
            pltpu.VMEM((rows, width), jnp.float32),
            pltpu.VMEM((inner, width), jnp.bfloat16),
            pltpu.VMEM((inner, width), jnp.bfloat16),
            pltpu.SemaphoreType.DMA((2, len(cuts))),
        ],
        compiler_params=pltpu.CompilerParams(vmem_limit_bytes=grant),
        cost_estimate=pl.CostEstimate(
            flops=6 * inner * width * rows, bytes_accessed=6 * inner * width, transcendentals=inner * rows
        ),
    )(perm, back, *parts, pg, pu, wg, wu, wd)


def weight_kernel(cuts, x_ref, g_ref, out_hbm, buf_ref, sems):
    x = x_ref[...]
    copies = []
    for at, (low, high) in enumerate(cuts):
        slot = at % SLOTS
        if at >= SLOTS:
            copies[at - SLOTS].wait()
        size = high - low
        buf_ref[slot, :size, :] = mm(g_ref[low:high, :], x, NN).astype(jnp.bfloat16)
        copies.append(
            pltpu.make_async_copy(buf_ref.at[slot, pl.ds(0, size), :], out_hbm.at[pl.ds(low, size), :], sems.at[slot])
        )
        copies[at].start()
    for copy in copies[max(0, len(copies) - SLOTS) :]:
        copy.wait()


def weight_call(x, g):
    inner, rows = g.shape
    width = x.shape[1]
    step = min(256, inner)
    cuts = cuts_of(inner, step)
    return pl.pallas_call(
        functools.partial(weight_kernel, cuts),
        in_specs=[pl.BlockSpec(memory_space=pltpu.VMEM)] * 2,
        out_specs=pl.BlockSpec(memory_space=pl.ANY),
        out_shape=jax.ShapeDtypeStruct((inner, width), jnp.bfloat16),
        scratch_shapes=[pltpu.VMEM((SLOTS, step, width), jnp.bfloat16), pltpu.SemaphoreType.DMA((SLOTS,))],
        compiler_params=pltpu.CompilerParams(vmem_limit_bytes=SMALL_MIB << 20),
        cost_estimate=pl.CostEstimate(
            flops=2 * inner * width * rows, bytes_accessed=2 * inner * width, transcendentals=0
        ),
    )(x, g)


def swap(value, axis, size, offset):
    rows = value.shape[0]
    spare = -rows % 8
    if spare:
        value = jnp.concatenate([value, jnp.zeros((spare,) + value.shape[1:], value.dtype)], axis=0)
    return lax.ppermute(value, axis, [(i, i ^ offset) for i in range(size)])[:rows]


def per_device(tokens, out_grad, routes, gate_probs, hot, gate_weight, up_weight, down_weight):
    groups = lax.axis_size("group")
    slices = lax.axis_size("ep")
    width = tokens.shape[1]
    half = width // 2
    block = groups * CAP
    bits = slices.bit_length() - 1
    order_a = list(range(bits - 1, -1, -1))
    order_b = [0] + list(range(bits - 1, 0, -1))
    masks_a, masks_b = masks_of(order_a), masks_of(order_b)

    experts = jnp.arange(groups, dtype=jnp.int32) ^ lax.axis_index("group")
    onehot, slot_weight = slot_map(routes, gate_probs, experts, CAP)
    hot_id = jnp.remainder(hot[0], groups)
    slot_ids = jnp.arange(CAP, dtype=jnp.int32)
    retained = ((experts == hot_id)[:, None] | (slot_ids[None, :] < COLD_CAP)).astype(jnp.float32)
    pick = onehot * retained[:, :, None]
    weight = slot_weight * retained
    picker = pick.astype(jnp.bfloat16)
    token_slots = jnp.einsum("est,td->esd", picker, tokens, preferred_element_type=jnp.float32).astype(jnp.bfloat16)
    picked = jnp.einsum("est,td->esd", picker, out_grad, preferred_element_type=jnp.float32)
    signal_slots = (weight[:, :, None] * picked).astype(jnp.bfloat16)
    def exchange(slots):
        own = jnp.concatenate([slots[0]] + [swap(slots[k], "group", groups, k) for k in range(1, groups)], axis=0)
        return (own[:, :half], own[:, half:])

    def send(held, stage):
        return tuple(swap(x, "ep", slices, 1 << order[stage]) for x, order in zip(held, (order_a, order_b)))

    def grow(held, got):
        return tuple(jnp.concatenate([x, y], axis=0) for x, y in zip(held, got))

    back = np.zeros((slices * block,) * 2, np.float32)
    for at, mask in enumerate(masks_b):
        for row in range(block):
            back[at * block + row, masks_a.index(mask) * block + row] = 1.0
    perm = jnp.asarray(back.T, jnp.bfloat16)
    back = jnp.asarray(back, jnp.bfloat16)

    wg = jnp.swapaxes(gate_weight[0], 0, 1)
    wu = jnp.swapaxes(up_weight[0], 0, 1)
    wd = down_weight[0]
    tie = lax.optimization_barrier

    held_t, held_s = exchange(token_slots), exchange(signal_slots)
    weights, loaded = [wg, wu], []
    held_t, weights = tie((held_t, weights))
    for stage in range(bits - 1):
        got_t = send(held_t, stage)
        if len(loaded) < 2:
            loaded.append(load_call(weights[len(loaded)], len(loaded)))
        held_t = grow(held_t, got_t)
        held_t, loaded, weights = tie((held_t, loaded, weights))
    held_t, held_s = tie((held_t, held_s))
    got_t = send(held_t, bits - 1)
    got_s = send(held_s, 0)
    for stage in range(1, bits - 2):
        held_s = grow(held_s, got_s)
        got_s = send(held_s, stage)
    held_s = grow(held_s, got_s)
    wg, wu_here = loaded
    held_t, got_t, held_s, wg, wu_here = tie((held_t, got_t, held_s, wg, wu_here))
    parts_t = (held_t[0], got_t[0], held_t[1], got_t[1])
    got_s = send(held_s, bits - 2)
    t, pg = gate_call(perm, parts_t, wg)
    held_s = grow(held_s, got_s)
    t, pg, held_s = tie((t, pg, held_s))
    got_s = send(held_s, bits - 1)
    pu = up_call(t, wu_here)
    pu, held_s, got_s = tie((pu, held_s, got_s))
    parts_s = (held_s[0], got_s[0], held_s[1], got_s[1])
    s, h, gs, us, keepa, senda, keepb, sendb = signal_call(perm, back, parts_s, pg, pu, wg, wu, wd)

    work = [(s, h), (t, gs), (t, us)]
    grads = []
    kept, sent = (keepa, keepb), (senda, sendb)
    for at, stage in enumerate(range(bits - 1, -1, -1)):
        got = send(sent, stage)
        if at < len(work):
            grads.append(weight_call(*work[at]))
        sums = tuple((x.astype(jnp.float32) + y.astype(jnp.float32)).astype(jnp.bfloat16) for x, y in zip(kept, got))
        sums, grads, work = tie((sums, grads, work))
        kept = tuple(x[: x.shape[0] // 2] for x in sums)
        sent = tuple(x[x.shape[0] // 2 :] for x in sums)
    for x, g in work[len(grads) :]:
        grads.append(weight_call(x, g))
    gd, gg, gu = grads
    dxa, dxb = sums
    mine = jnp.concatenate([dxa, dxb], axis=1).reshape(groups, CAP, width)
    returned = jnp.stack([mine[0]] + [swap(mine[k], "group", groups, k) for k in range(1, groups)])
    tokens_grad = jnp.einsum("est,esd->td", picker, returned, preferred_element_type=jnp.float32).astype(jnp.bfloat16)
    return (tokens_grad, jnp.swapaxes(gg, 0, 1)[None], jnp.swapaxes(gu, 0, 1)[None], gd[None])


def solution(mesh):
    in_specs = (
        P(("group", "ep"), None),
        P(("group", "ep"), None),
        P(("group", "ep"), None),
        P(("group", "ep"), None),
        P(),
        P("group", None, "ep"),
        P("group", None, "ep"),
        P("group", "ep", None),
    )
    out_specs = (
        P(("group", "ep"), None),
        P("group", None, "ep"),
        P("group", None, "ep"),
        P("group", "ep", None),
    )
    return jax.shard_map(per_device, mesh=mesh, in_specs=in_specs, out_specs=out_specs, check_vma=False)
```

time: 144 us -> 116 us (0.81)
  waiting for transfers between devices: 54.2 us -> 28.9 us
  Pallas kernels: 53.8 us -> 48.2 us
  starting transfers between devices: 25.4 us -> 30.6 us
  local copies, waits for them, and re-layouts: 3.07 us -> 0.47 us
    ppermute x18 -> x27, waiting for transfers between devices: 54.2 us -> 28.9 us  [swap(): lax.ppermute(value, axis, [(i, i ^ offset) for i in range(size)])[:rows]]
    pallas_call x4 -> x8, Pallas kernels: 53.8 us -> 48.2 us  [the longest x1 18.3 us: signal_call(): pl.pallas_call(functools.partial(signal_kernel, cuts), in_specs=[VMEM] *...]
    ppermute x18 -> x27, starting transfers between devices: 25.4 us -> 30.6 us  [swap(): lax.ppermute(value, axis, [(i, i ^ offset) for i in range(size)])[:rows]]
    slice x7, local copies, waits for them, and re-layouts: 2.19 us -> 0.16 us  [the longest x4 0.08 us: per_device(): sent = tuple((x[x.shape[0] // 2:] for x in sums))]
  transfers between devices with their start and end apart: 18 -> 27, of which waited for: 11 -> 17; matrix products, arithmetic and copies ran while one was open for 1% -> 3% of each run, Pallas kernels for 10% -> 26%
where the time goes in v2:
time: 116 us
  Pallas kernels  48.2 us (42%)
  starting transfers between devices  30.6 us (26%)
  waiting for transfers between devices  28.9 us (25%)
  matrix products  3.38 us (3%)
  other arithmetic  2.87 us (2%)
  between operations  1.87 us (2%)
    ppermute x27, starting transfers between devices, swap(): lax.ppermute(value, axis, [(i, i ^ offset) for i in range(size)])[:rows]  30.6 us
    ppermute x27, waiting for transfers between devices, swap(): lax.ppermute(value, axis, [(i, i ^ offset) for i in range(size)])[:rows]  28.9 us
    pallas_call x1, Pallas kernels, signal_call(): pl.pallas_call(functools.partial(signal_kernel, cuts), in_specs=[VMEM] *...  18.3 us
    pallas_call x3, Pallas kernels, weight_call(): pl.pallas_call(functools.partial(weight_kernel, cuts), in_specs=[pl.Block...  14.9 us
    pallas_call x2, Pallas kernels, load_call(): pl.pallas_call(functools.partial(load_kernel, cuts), in_specs=[pl.BlockSp...  8.64 us
    pallas_call x1, Pallas kernels, gate_call(): pl.pallas_call(functools.partial(gate_kernel, cuts_of(inner, STEP)), in_s...  3.22 us
    pallas_call x1, Pallas kernels, up_call(): pl.pallas_call(functools.partial(up_kernel, cuts_of(inner, STEP)), in_spe...  3.08 us
  transfers between devices with their start and end apart: 27, of which 17 were waited for; matrix products, arithmetic and copies ran while one was open for 3% of the time, Pallas kernels for 26%

profile of v2, /device:TPU:0, one launch (start us, length us, event | category | flops | bytes accessed | tf_op | source)
XLA Modules:
  0.0 116.2 jit_solution(658723480458319461)
XLA Ops:
  3.6 2.6 %collective-permute-start.1 = (bf16[8,4096]{1,0:T(8,128)(2,1)S(1)}, bf16[8,4096]{1,0:T(8,128)(2,1)S(1)}, u32[]{:S(2)}, u32[]{:S(2)}) collective-permute-start(bf16[8,4096]{1,0:T(8,128)(2,1)S(1)} %concatenate.79), channel_id=1, source_target_pairs={{0,16},{8,24},{16,0},{24,8},{1,17},{9,25},{17,1},{25,9},{2,18},{10... | collective-permute-start | bytes 196616 | tf_op jit(solution)/shard_map/ppermute | solution.py:257
  9.0 2.0 %collective-permute-start.8 = (bf16[8,4096]{1,0:T(8,128)(2,1)S(1)}, bf16[8,4096]{1,0:T(8,128)(2,1)S(1)}, u32[]{:S(2)}, u32[]{:S(2)}) collective-permute-start(bf16[8,4096]{1,0:T(8,128)(2,1)S(1)} %concatenate.89), channel_id=1, source_target_pairs={{0,16},{8,24},{16,0},{24,8},{1,17},{9,25},{17,1},{25,9},{2,18},{10... | collective-permute-start | bytes 196616 | tf_op jit(solution)/shard_map/ppermute | solution.py:257
  13.0 2.6 %collective-permute-start.3 = (bf16[24,2048]{1,0:T(8,128)(2,1)S(1)}, bf16[24,2048]{1,0:T(8,128)(2,1)S(1)}, u32[]{:S(2)}, u32[]{:S(2)}) collective-permute-start(bf16[24,2048]{1,0:T(8,128)(2,1)S(1)} %concatenate.82), channel_id=1, source_target_pairs={{0,4},{1,5},{2,6},{3,7},{4,0},{5,1},{6,2},{7,3},{8,12},{9,13},{10,... | collective-permute-start | bytes 294920 | tf_op jit(solution)/shard_map/ppermute | solution.py:257
  15.7 4.3 %shard_map.129.wg_ref = bf16[1376,4096]{1,0:T(8,128)(2,1)S(1)} custom-call(bf16[1376,4096]{1,0:T(8,128)(2,1)} %bitcast.67), custom_call_target="tpu_custom_call" | custom-call | bytes 11272192 | tf_op jit(solution)/shard_map/pallas_call | solution.py:89
  21.8 3.4 %collective-permute-start.6 = (bf16[40,2048]{1,0:T(8,128)(2,1)S(1)}, bf16[40,2048]{1,0:T(8,128)(2,1)S(1)}, u32[]{:S(2)}, u32[]{:S(2)}) collective-permute-start(bf16[40,2048]{1,0:T(8,128)(2,1)S(1)} %pad_maximum_fusion.7), channel_id=1, source_target_pairs={{0,4},{1,5},{2,6},{3,7},{4,0},{5,1},{6,2},{7,3},{8,12},{9,13},{10,... | collective-permute-start | bytes 491528 | tf_op jit(solution)/shard_map/ppermute | solution.py:257
  25.2 4.3 %shard_map.130.wu_ref = bf16[1376,4096]{1,0:T(8,128)(2,1)S(1)} custom-call(bf16[1376,4096]{1,0:T(8,128)(2,1)} %bitcast.62), custom_call_target="tpu_custom_call" | custom-call | bytes 11272192 | tf_op jit(solution)/shard_map/pallas_call | solution.py:89
  29.8 3.1 %collective-permute-done.6 = bf16[40,2048]{1,0:T(8,128)(2,1)S(1)} collective-permute-done((bf16[40,2048]{1,0:T(8,128)(2,1)S(1)}, bf16[40,2048]{1,0:T(8,128)(2,1)S(1)}, u32[]{:S(2)}, u32[]{:S(2)}) %collective-permute-start.6) | collective-permute-done | bytes 163872 | tf_op jit(solution)/shard_map/ppermute | solution.py:257
  35.2 2.9 %collective-permute-start.11 = (bf16[80,2048]{1,0:T(8,128)(2,1)S(1)}, bf16[80,2048]{1,0:T(8,128)(2,1)S(1)}, u32[]{:S(2)}, u32[]{:S(2)}) collective-permute-start(bf16[80,2048]{1,0:T(8,128)(2,1)S(1)} %pad_maximum_fusion.1.b0_ref), channel_id=1, source_target_pairs={{0,2},{1,3},{2,0},{3,1},{4,6},{5,7},{6,4},{7,5},{8,10},{9,11},{10,... | collective-permute-start | bytes 983048 | tf_op jit(solution)/shard_map/ppermute | solution.py:257
  38.7 1.8 %collective-permute-done.12 = bf16[24,2048]{1,0:T(8,128)(2,1)S(1)} collective-permute-done((bf16[24,2048]{1,0:T(8,128)(2,1)S(1)}, bf16[24,2048]{1,0:T(8,128)(2,1)S(1)}, u32[]{:S(2)}, u32[]{:S(2)}) %collective-permute-start.12) | collective-permute-done | bytes 98336 | tf_op jit(solution)/shard_map/ppermute | solution.py:257
  40.5 3.0 %collective-permute-done.10.a1_ref = bf16[80,2048]{1,0:T(8,128)(2,1)S(1)} collective-permute-done((bf16[80,2048]{1,0:T(8,128)(2,1)S(1)}, bf16[80,2048]{1,0:T(8,128)(2,1)S(1)}, u32[]{:S(2)}, u32[]{:S(2)}) %collective-permute-start.10) | collective-permute-done | bytes 327712 | tf_op jit(solution)/shard_map/ppermute | solution.py:257
  43.6 1.8 %collective-permute-done.11.b1_ref = bf16[80,2048]{1,0:T(8,128)(2,1)S(1)} collective-permute-done((bf16[80,2048]{1,0:T(8,128)(2,1)S(1)}, bf16[80,2048]{1,0:T(8,128)(2,1)S(1)}, u32[]{:S(2)}, u32[]{:S(2)}) %collective-permute-start.11) | collective-permute-done | bytes 327712 | tf_op jit(solution)/shard_map/ppermute | solution.py:257
  46.0 2.4 %collective-permute-start.15 = (bf16[40,2048]{1,0:T(8,128)(2,1)S(1)}, bf16[40,2048]{1,0:T(8,128)(2,1)S(1)}, u32[]{:S(2)}, u32[]{:S(2)}) collective-permute-start(bf16[40,2048]{1,0:T(8,128)(2,1)S(1)} %pad_maximum_fusion.9), channel_id=1, source_target_pairs={{0,4},{1,5},{2,6},{3,7},{4,0},{5,1},{6,2},{7,3},{8,12},{9,13},{10,... | collective-permute-start | bytes 491528 | tf_op jit(solution)/shard_map/ppermute | solution.py:257
  48.4 3.2 %shard_map.131 = (bf16[160,4096]{1,0:T(8,128)(2,1)S(1)}, f32[1376,160]{1,0:T(8,128)S(1)}) custom-call(bf16[160,160]{1,0:T(8,128)(2,1)S(1)} %copy-done.3, bf16[80,2048]{1,0:T(8,128)(2,1)S(1)} %pad_maximum_fusion.a0_ref, bf16[80,2048]{1,0:T(8,128)(2,1)S(1)} %collective-permute-done.10.a1_ref, bf16[80,2048]{1,0:T(8,128)(2,1)S(1)} %pad_maximum_fusion.1.b0_ref, ...), custom_call_target="tpu_custom_call" | custom-call | flops 1803550720 | bytes 11272192 | tf_op jit(solution)/shard_map/pallas_call | solution.py:110
  52.7 2.6 %collective-permute-done.15 = bf16[40,2048]{1,0:T(8,128)(2,1)S(1)} collective-permute-done((bf16[40,2048]{1,0:T(8,128)(2,1)S(1)}, bf16[40,2048]{1,0:T(8,128)(2,1)S(1)}, u32[]{:S(2)}, u32[]{:S(2)}) %collective-permute-start.15) | collective-permute-done | bytes 163872 | tf_op jit(solution)/shard_map/ppermute | solution.py:257
  56.2 3.1 %shard_map.132.pu_ref = f32[1376,160]{1,0:T(8,128)S(1)} custom-call(bf16[160,4096]{1,0:T(8,128)(2,1)S(1)} %get-tuple-element.119.t_ref.x_ref, bf16[1376,4096]{1,0:T(8,128)(2,1)S(1)} %shard_map.130.wu_ref), custom_call_target="tpu_custom_call" | custom-call | flops 1803550720 | bytes 11272192 | tf_op jit(solution)/shard_map/pallas_call | solution.py:134
  59.3 3.2 %collective-permute-done.16.a1_ref = bf16[80,2048]{1,0:T(8,128)(2,1)S(1)} collective-permute-done((bf16[80,2048]{1,0:T(8,128)(2,1)S(1)}, bf16[80,2048]{1,0:T(8,128)(2,1)S(1)}, u32[]{:S(2)}, u32[]{:S(2)}) %collective-permute-start.16) | collective-permute-done | bytes 327712 | tf_op jit(solution)/shard_map/ppermute | solution.py:257
  63.2 18.3 %shard_map.133 = (bf16[160,4096]{1,0:T(8,128)(2,1)S(1)}, bf16[1376,160]{1,0:T(8,128)(2,1)S(1)}, bf16[1376,160]{1,0:T(8,128)(2,1)S(1)}, bf16[1376,160]{1,0:T(8,12...) custom-call(bf16[160,160]{1,0:T(8,128)(2,1)S(1)} %copy-done.3, ...), custom_call_target="tpu_custom_call" | custom-call | flops 5410652160 | bytes 33816576 | tf_op jit(solution)/shard_map/pallas_call | solution.py:197
  83.5 4.9 %shard_map.134 = bf16[1376,4096]{1,0:T(8,128)(2,1)} custom-call(bf16[160,4096]{1,0:T(8,128)(2,1)S(1)} %get-tuple-element.104.x_ref, bf16[1376,160]{1,0:T(8,128)(2,1)S(1)} %get-tuple-element.105.g_ref), custom_call_target="tpu_custom_call" | custom-call | flops 1803550720 | bytes 11272192 | tf_op jit(solution)/shard_map/pallas_call | solution.py:239
  88.7 4.1 %collective-permute-done.19 = bf16[80,2048]{1,0:T(8,128)(2,1)S(1)} collective-permute-done((bf16[80,2048]{1,0:T(8,128)(2,1)S(1)}, bf16[80,2048]{1,0:T(8,128)(2,1)S(1)}, u32[]{:S(2)}, u32[]{:S(2)}) %collective-permute-start.19) | collective-permute-done | bytes 327712 | tf_op jit(solution)/shard_map/ppermute | solution.py:257
  93.0 2.6 %collective-permute-start.20 = (bf16[40,2048]{1,0:T(8,128)(2,1)S(1)}, bf16[40,2048]{1,0:T(8,128)(2,1)S(1)}, u32[]{:S(2)}, u32[]{:S(2)}) collective-permute-start(bf16[40,2048]{1,0:T(8,128)(2,1)S(1)} %slice.146), channel_id=1, source_target_pairs={{0,2},{1,3},{2,0},{3,1},{4,6},{5,7},{6,4},{7,5},{8,10},{9,11},{10,... | collective-permute-start | bytes 491528 | tf_op jit(solution)/shard_map/ppermute | solution.py:257
  95.6 4.9 %shard_map.135 = bf16[1376,4096]{1,0:T(8,128)(2,1)} custom-call(bf16[160,4096]{1,0:T(8,128)(2,1)S(1)} %get-tuple-element.119.t_ref.x_ref, bf16[1376,160]{1,0:T(8,128)(2,1)S(1)} %get-tuple-element.112.g_ref), custom_call_target="tpu_custom_call" | custom-call | flops 1803550720 | bytes 11272192 | tf_op jit(solution)/shard_map/pallas_call | solution.py:239
  100.6 1.6 %collective-permute-done.21 = bf16[40,2048]{1,0:T(8,128)(2,1)S(1)} collective-permute-done((bf16[40,2048]{1,0:T(8,128)(2,1)S(1)}, bf16[40,2048]{1,0:T(8,128)(2,1)S(1)}, u32[]{:S(2)}, u32[]{:S(2)}) %collective-permute-start.21) | collective-permute-done | bytes 163872 | tf_op jit(solution)/shard_map/ppermute | solution.py:257
  103.4 5.0 %shard_map.136 = bf16[1376,4096]{1,0:T(8,128)(2,1)} custom-call(bf16[160,4096]{1,0:T(8,128)(2,1)S(1)} %get-tuple-element.119.t_ref.x_ref, bf16[1376,160]{1,0:T(8,128)(2,1)S(1)} %get-tuple-element.120.g_ref), custom_call_target="tpu_custom_call" | custom-call | flops 1803550720 | bytes 11272192 | tf_op jit(solution)/shard_map/pallas_call | solution.py:239
  111.1 3.1 %collective-permute-done.25 = bf16[8,4096]{1,0:T(8,128)(2,1)S(1)} collective-permute-done((bf16[8,4096]{1,0:T(8,128)(2,1)S(1)}, bf16[8,4096]{1,0:T(8,128)(2,1)S(1)}, u32[]{:S(2)}, u32[]{:S(2)}) %collective-permute-start.25) | collective-permute-done | bytes 65568 | tf_op jit(solution)/shard_map/ppermute | solution.py:257
  (107 shorter events, 23.3 us)
Async XLA Ops:
  3.0 8.1 %collective-permute-start = (bf16[8,4096]{1,0:T(8,128)(2,1)S(1)}, bf16[8,4096]{1,0:T(8,128)(2,1)S(1)}, u32[]{:S(2)}, u32[]{:S(2)}) collective-permute-start(bf16[8,4096]{1,0:T(8,128)(2,1)S(1)} %concatenate.78), channel_id=1, source_target_pairs={{0,8},{8,0},{16,24},{24,16},{1,9},{9,1},{17,25},{25,17},{2,10},{10... | collective-permute-start | bytes 196616 | tf_op jit(solution)/shard_map/ppermute | solution.py:257
  3.6 7.6 %collective-permute-start.1 = (bf16[8,4096]{1,0:T(8,128)(2,1)S(1)}, bf16[8,4096]{1,0:T(8,128)(2,1)S(1)}, u32[]{:S(2)}, u32[]{:S(2)}) collective-permute-start(bf16[8,4096]{1,0:T(8,128)(2,1)S(1)} %concatenate.79), channel_id=1, source_target_pairs={{0,16},{8,24},{16,0},{24,8},{1,17},{9,25},{17,1},{25,9},{2,18},{10... | collective-permute-start | bytes 196616 | tf_op jit(solution)/shard_map/ppermute | solution.py:257
  6.1 5.0 %collective-permute-start.2 = (bf16[8,4096]{1,0:T(8,128)(2,1)S(1)}, bf16[8,4096]{1,0:T(8,128)(2,1)S(1)}, u32[]{:S(2)}, u32[]{:S(2)}) collective-permute-start(bf16[8,4096]{1,0:T(8,128)(2,1)S(1)} %concatenate.80), channel_id=1, source_target_pairs={{0,24},{8,16},{16,8},{24,0},{1,25},{9,17},{17,9},{25,1},{2,26},{10... | collective-permute-start | bytes 196616 | tf_op jit(solution)/shard_map/ppermute | solution.py:257
  8.8 6.7 %collective-permute-start.7 = (bf16[8,4096]{1,0:T(8,128)(2,1)S(1)}, bf16[8,4096]{1,0:T(8,128)(2,1)S(1)}, u32[]{:S(2)}, u32[]{:S(2)}) collective-permute-start(bf16[8,4096]{1,0:T(8,128)(2,1)S(1)} %concatenate.88), channel_id=1, source_target_pairs={{0,8},{8,0},{16,24},{24,16},{1,9},{9,1},{17,25},{25,17},{2,10},{10... | collective-permute-start | bytes 196616 | tf_op jit(solution)/shard_map/ppermute | solution.py:257
  9.0 6.5 %collective-permute-start.8 = (bf16[8,4096]{1,0:T(8,128)(2,1)S(1)}, bf16[8,4096]{1,0:T(8,128)(2,1)S(1)}, u32[]{:S(2)}, u32[]{:S(2)}) collective-permute-start(bf16[8,4096]{1,0:T(8,128)(2,1)S(1)} %concatenate.89), channel_id=1, source_target_pairs={{0,16},{8,24},{16,0},{24,8},{1,17},{9,25},{17,1},{25,9},{2,18},{10... | collective-permute-start | bytes 196616 | tf_op jit(solution)/shard_map/ppermute | solution.py:257
  11.3 8.7 %collective-permute-start.4 = (bf16[24,2048]{1,0:T(8,128)(2,1)S(1)}, bf16[24,2048]{1,0:T(8,128)(2,1)S(1)}, u32[]{:S(2)}, u32[]{:S(2)}) collective-permute-start(bf16[24,2048]{1,0:T(8,128)(2,1)S(1)} %concatenate.84), channel_id=1, source_target_pairs={{0,1},{1,0},{2,3},{3,2},{4,5},{5,4},{6,7},{7,6},{8,9},{9,8},{10,11... | collective-permute-start | bytes 294920 | tf_op jit(solution)/shard_map/ppermute | solution.py:257
  13.0 8.0 %collective-permute-start.3 = (bf16[24,2048]{1,0:T(8,128)(2,1)S(1)}, bf16[24,2048]{1,0:T(8,128)(2,1)S(1)}, u32[]{:S(2)}, u32[]{:S(2)}) collective-permute-start(bf16[24,2048]{1,0:T(8,128)(2,1)S(1)} %concatenate.82), channel_id=1, source_target_pairs={{0,4},{1,5},{2,6},{3,7},{4,0},{5,1},{6,2},{7,3},{8,12},{9,13},{10,... | collective-permute-start | bytes 294920 | tf_op jit(solution)/shard_map/ppermute | solution.py:257
  21.0 8.8 %collective-permute-start.5 = (bf16[40,2048]{1,0:T(8,128)(2,1)S(1)}, bf16[40,2048]{1,0:T(8,128)(2,1)S(1)}, u32[]{:S(2)}, u32[]{:S(2)}) collective-permute-start(bf16[40,2048]{1,0:T(8,128)(2,1)S(1)} %pad_maximum_fusion.6), channel_id=1, source_target_pairs={{0,2},{1,3},{2,0},{3,1},{4,6},{5,7},{6,4},{7,5},{8,10},{9,11},{10,... | collective-permute-start | bytes 491528 | tf_op jit(solution)/shard_map/ppermute | solution.py:257
  21.8 11.1 %collective-permute-start.6 = (bf16[40,2048]{1,0:T(8,128)(2,1)S(1)}, bf16[40,2048]{1,0:T(8,128)(2,1)S(1)}, u32[]{:S(2)}, u32[]{:S(2)}) collective-permute-start(bf16[40,2048]{1,0:T(8,128)(2,1)S(1)} %pad_maximum_fusion.7), channel_id=1, source_target_pairs={{0,4},{1,5},{2,6},{3,7},{4,0},{5,1},{6,2},{7,3},{8,12},{9,13},{10,... | collective-permute-start | bytes 491528 | tf_op jit(solution)/shard_map/ppermute | solution.py:257
  32.9 5.7 %collective-permute-start.13 = (bf16[24,2048]{1,0:T(8,128)(2,1)S(1)}, bf16[24,2048]{1,0:T(8,128)(2,1)S(1)}, u32[]{:S(2)}, u32[]{:S(2)}) collective-permute-start(bf16[24,2048]{1,0:T(8,128)(2,1)S(1)} %concatenate.94), channel_id=1, source_target_pairs={{0,1},{1,0},{2,3},{3,2},{4,5},{5,4},{6,7},{7,6},{8,9},{9,8},{10,11... | collective-permute-start | bytes 294920 | tf_op jit(solution)/shard_map/ppermute | solution.py:257
  33.8 6.6 %collective-permute-start.12 = (bf16[24,2048]{1,0:T(8,128)(2,1)S(1)}, bf16[24,2048]{1,0:T(8,128)(2,1)S(1)}, u32[]{:S(2)}, u32[]{:S(2)}) collective-permute-start(bf16[24,2048]{1,0:T(8,128)(2,1)S(1)} %concatenate.92), channel_id=1, source_target_pairs={{0,4},{1,5},{2,6},{3,7},{4,0},{5,1},{6,2},{7,3},{8,12},{9,13},{10,... | collective-permute-start | bytes 294920 | tf_op jit(solution)/shard_map/ppermute | solution.py:257
  34.2 9.4 %collective-permute-start.10 = (bf16[80,2048]{1,0:T(8,128)(2,1)S(1)}, bf16[80,2048]{1,0:T(8,128)(2,1)S(1)}, u32[]{:S(2)}, u32[]{:S(2)}) collective-permute-start(bf16[80,2048]{1,0:T(8,128)(2,1)S(1)} %pad_maximum_fusion.a0_ref), channel_id=1, source_target_pairs={{0,1},{1,0},{2,3},{3,2},{4,5},{5,4},{6,7},{7,6},{8,9},{9,8},{10,11... | collective-permute-start | bytes 983048 | tf_op jit(solution)/shard_map/ppermute | solution.py:257
  35.2 10.1 %collective-permute-start.11 = (bf16[80,2048]{1,0:T(8,128)(2,1)S(1)}, bf16[80,2048]{1,0:T(8,128)(2,1)S(1)}, u32[]{:S(2)}, u32[]{:S(2)}) collective-permute-start(bf16[80,2048]{1,0:T(8,128)(2,1)S(1)} %pad_maximum_fusion.1.b0_ref), channel_id=1, source_target_pairs={{0,2},{1,3},{2,0},{3,1},{4,6},{5,7},{6,4},{7,5},{8,10},{9,11},{10,... | collective-permute-start | bytes 983048 | tf_op jit(solution)/shard_map/ppermute | solution.py:257
  45.3 7.3 %collective-permute-start.14 = (bf16[40,2048]{1,0:T(8,128)(2,1)S(1)}, bf16[40,2048]{1,0:T(8,128)(2,1)S(1)}, u32[]{:S(2)}, u32[]{:S(2)}) collective-permute-start(bf16[40,2048]{1,0:T(8,128)(2,1)S(1)} %pad_maximum_fusion.8), channel_id=1, source_target_pairs={{0,2},{1,3},{2,0},{3,1},{4,6},{5,7},{6,4},{7,5},{8,10},{9,11},{10,... | collective-permute-start | bytes 491528 | tf_op jit(solution)/shard_map/ppermute | solution.py:257
  46.0 9.3 %collective-permute-start.15 = (bf16[40,2048]{1,0:T(8,128)(2,1)S(1)}, bf16[40,2048]{1,0:T(8,128)(2,1)S(1)}, u32[]{:S(2)}, u32[]{:S(2)}) collective-permute-start(bf16[40,2048]{1,0:T(8,128)(2,1)S(1)} %pad_maximum_fusion.9), channel_id=1, source_target_pairs={{0,4},{1,5},{2,6},{3,7},{4,0},{5,1},{6,2},{7,3},{8,12},{9,13},{10,... | collective-permute-start | bytes 491528 | tf_op jit(solution)/shard_map/ppermute | solution.py:257
  55.4 7.1 %collective-permute-start.16 = (bf16[80,2048]{1,0:T(8,128)(2,1)S(1)}, bf16[80,2048]{1,0:T(8,128)(2,1)S(1)}, u32[]{:S(2)}, u32[]{:S(2)}) collective-permute-start(bf16[80,2048]{1,0:T(8,128)(2,1)S(1)} %pad_maximum_fusion.2.a0_ref), channel_id=1, source_target_pairs={{0,1},{1,0},{2,3},{3,2},{4,5},{5,4},{6,7},{7,6},{8,9},{9,8},{10,11... | collective-permute-start | bytes 983048 | tf_op jit(solution)/shard_map/ppermute | solution.py:257
  56.1 7.1 %collective-permute-start.17 = (bf16[80,2048]{1,0:T(8,128)(2,1)S(1)}, bf16[80,2048]{1,0:T(8,128)(2,1)S(1)}, u32[]{:S(2)}, u32[]{:S(2)}) collective-permute-start(bf16[80,2048]{1,0:T(8,128)(2,1)S(1)} %pad_maximum_fusion.3.b0_ref), channel_id=1, source_target_pairs={{0,2},{1,3},{2,0},{3,1},{4,6},{5,7},{6,4},{7,5},{8,10},{9,11},{10,... | collective-permute-start | bytes 983048 | tf_op jit(solution)/shard_map/ppermute | solution.py:257
  81.5 7.1 %collective-permute-start.18 = (bf16[80,2048]{1,0:T(8,128)(2,1)S(1)}, bf16[80,2048]{1,0:T(8,128)(2,1)S(1)}, u32[]{:S(2)}, u32[]{:S(2)}) collective-permute-start(bf16[80,2048]{1,0:T(8,128)(2,1)S(1)} %get-tuple-element.101), channel_id=1, source_target_pairs={{0,1},{1,0},{2,3},{3,2},{4,5},{5,4},{6,7},{7,6},{8,9},{9,8},{10,11... | collective-permute-start | bytes 983048 | tf_op jit(solution)/shard_map/ppermute | solution.py:257
  82.9 9.9 %collective-permute-start.19 = (bf16[80,2048]{1,0:T(8,128)(2,1)S(1)}, bf16[80,2048]{1,0:T(8,128)(2,1)S(1)}, u32[]{:S(2)}, u32[]{:S(2)}) collective-permute-start(bf16[80,2048]{1,0:T(8,128)(2,1)S(1)} %get-tuple-element.103), channel_id=1, source_target_pairs={{0,2},{1,3},{2,0},{3,1},{4,6},{5,7},{6,4},{7,5},{8,10},{9,11},{10,... | collective-permute-start | bytes 983048 | tf_op jit(solution)/shard_map/ppermute | solution.py:257
  92.9 9.3 %collective-permute-start.21 = (bf16[40,2048]{1,0:T(8,128)(2,1)S(1)}, bf16[40,2048]{1,0:T(8,128)(2,1)S(1)}, u32[]{:S(2)}, u32[]{:S(2)}) collective-permute-start(bf16[40,2048]{1,0:T(8,128)(2,1)S(1)} %slice.148), channel_id=1, source_target_pairs={{0,4},{1,5},{2,6},{3,7},{4,0},{5,1},{6,2},{7,3},{8,12},{9,13},{10,... | collective-permute-start | bytes 491528 | tf_op jit(solution)/shard_map/ppermute | solution.py:257
  93.0 9.3 %collective-permute-start.20 = (bf16[40,2048]{1,0:T(8,128)(2,1)S(1)}, bf16[40,2048]{1,0:T(8,128)(2,1)S(1)}, u32[]{:S(2)}, u32[]{:S(2)}) collective-permute-start(bf16[40,2048]{1,0:T(8,128)(2,1)S(1)} %slice.146), channel_id=1, source_target_pairs={{0,2},{1,3},{2,0},{3,1},{4,6},{5,7},{6,4},{7,5},{8,10},{9,11},{10,... | collective-permute-start | bytes 491528 | tf_op jit(solution)/shard_map/ppermute | solution.py:257
  102.4 6.0 %collective-permute-start.23 = (bf16[24,2048]{1,0:T(8,128)(2,1)S(1)}, bf16[24,2048]{1,0:T(8,128)(2,1)S(1)}, u32[]{:S(2)}, u32[]{:S(2)}) collective-permute-start(bf16[24,2048]{1,0:T(8,128)(2,1)S(1)} %concatenate.99), channel_id=1, source_target_pairs={{0,1},{1,0},{2,3},{3,2},{4,5},{5,4},{6,7},{7,6},{8,9},{9,8},{10,11... | collective-permute-start | bytes 294920 | tf_op jit(solution)/shard_map/ppermute | solution.py:257
  103.4 5.5 %collective-permute-start.22 = (bf16[24,2048]{1,0:T(8,128)(2,1)S(1)}, bf16[24,2048]{1,0:T(8,128)(2,1)S(1)}, u32[]{:S(2)}, u32[]{:S(2)}) collective-permute-start(bf16[24,2048]{1,0:T(8,128)(2,1)S(1)} %concatenate.98), channel_id=1, source_target_pairs={{0,4},{1,5},{2,6},{3,7},{4,0},{5,1},{6,2},{7,3},{8,12},{9,13},{10,... | collective-permute-start | bytes 294920 | tf_op jit(solution)/shard_map/ppermute | solution.py:257
  109.2 5.0 %collective-permute-start.25 = (bf16[8,4096]{1,0:T(8,128)(2,1)S(1)}, bf16[8,4096]{1,0:T(8,128)(2,1)S(1)}, u32[]{:S(2)}, u32[]{:S(2)}) collective-permute-start(bf16[8,4096]{1,0:T(8,128)(2,1)S(1)} %concatenate.102), channel_id=1, source_target_pairs={{0,16},{8,24},{16,0},{24,8},{1,17},{9,25},{17,1},{25,9},{2,18},{10... | collective-permute-start | bytes 196616 | tf_op jit(solution)/shard_map/ppermute | solution.py:257
  (8 other events, 111.5 us)

commit v3 on v2

--- a/solution.py
+++ b/solution.py
@@ -12,9 +12,9 @@
 COLD_CAP = 3
 SLOTS = 3
 STEP = 512
-BANDS = 4
+AHEAD = 4
+SIGNAL_MIB = 44
 SMALL_MIB = 12
-SPARE_MIB = 16
 
 NT = (((1,), (1,)), ((), ()))
 TN = (((0,), (0,)), ((), ()))
@@ -144,70 +144,83 @@
 
 
 def signal_kernel(
-    cuts, perm_ref, back_ref, a0_ref, a1_ref, b0_ref, b1_ref, pg_ref, pu_ref, wg_ref, wu_hbm, wd_hbm,
-    s_ref, h_ref, gs_ref, us_ref, keepa_ref, senda_ref, keepb_ref, sendb_ref, acc_ref, wu_ref, wd_ref, sems,
+    cuts, perm_ref, back_ref, a0_ref, a1_ref, b0_ref, b1_ref, pg_ref, pu_ref, wg_hbm, wu_hbm, wd_hbm,
+    s_ref, h_ref, gs_ref, us_ref, keepa_ref, senda_ref, keepb_ref, sendb_ref, both_ref, w_ref, wd_ref, acc_ref, sems,
 ):
     copies = []
-    for side, (src, dst) in enumerate(((wd_hbm, wd_ref), (wu_hbm, wu_ref))):
-        for at, (low, high) in enumerate(cuts):
-            rows = pl.ds(low, high - low)
-            copies.append(pltpu.make_async_copy(src.at[rows, :], dst.at[rows, :], sems.at[side, at]))
-    for copy in copies[: len(cuts)]:
+    for at, (low, high) in enumerate(cuts):
+        rows = pl.ds(low, high - low)
+        copies.append(pltpu.make_async_copy(wd_hbm.at[rows, :], wd_ref.at[rows, :], sems.at[0, at]))
+    for at, (low, high) in enumerate(cuts):
+        size = high - low
+        for side, src in enumerate((wg_hbm, wu_hbm)):
+            dst = w_ref.at[pl.ds(2 * low + side * size, size), :]
+            copies.append(pltpu.make_async_copy(src.at[pl.ds(low, size), :], dst, sems.at[1 + side, at]))
+    for copy in copies[:AHEAD]:
         copy.start()
-    s = join(perm_ref[...], (a0_ref, a1_ref, b0_ref, b1_ref))
-    s_ref[...] = s
-    for at, (low, high) in enumerate(cuts):
+
+    def arrive(at):
+        copies[at].wait()
+        if at + AHEAD < len(copies):
+            copies[at + AHEAD].start()
+
+    s_ref[...] = join(perm_ref[...], (a0_ref, a1_ref, b0_ref, b1_ref))
+    s = s_ref[...]
+    for at, (low, high) in enumerate(cuts):
+        size = high - low
         gate = pg_ref[low:high, :]
         up = pu_ref[low:high, :]
         logistic = jax.nn.sigmoid(gate)
         swished = gate * logistic
         h_ref[low:high, :] = (swished * up).astype(jnp.bfloat16)
-        copies[at].wait()
-        copies[len(cuts) + at].start()
+        arrive(at)
         hidden_grad = mm(wd_ref[low:high, :], s, NT)
-        gs_ref[low:high, :] = (hidden_grad * up * logistic * (1.0 + gate * (1.0 - logistic))).astype(jnp.bfloat16)
-        us_ref[low:high, :] = (hidden_grad * swished).astype(jnp.bfloat16)
+        gs = (hidden_grad * up * logistic * (1.0 + gate * (1.0 - logistic))).astype(jnp.bfloat16)
+        us = (hidden_grad * swished).astype(jnp.bfloat16)
+        gs_ref[low:high, :] = gs
+        us_ref[low:high, :] = us
+        both_ref[2 * low : 2 * low + size, :] = gs
+        both_ref[2 * low + size : 2 * high, :] = us
     half = keepa_ref.shape[1]
     kept = keepa_ref.shape[0]
-    wide = 2 * half // BANDS
-    bands = [slice(band * wide, (band + 1) * wide) for band in range(BANDS)]
-    gs = gs_ref[...].T
-    for cols in bands:
-        acc_ref[:, cols] = mm(gs, wg_ref[:, cols], NN)
-    us = us_ref[...].T
-    for copy in copies[len(cuts) :]:
-        copy.wait()
-    for cols in bands:
-        part = (acc_ref[:, cols] + mm(us, wu_ref[:, cols], NN)).astype(jnp.bfloat16)
-        if cols.start < half:
-            keepa_ref[:, cols] = part[:kept]
-            senda_ref[:, cols] = part[kept:]
+    for at, (low, high) in enumerate(cuts):
+        arrive(len(cuts) + 2 * at)
+        arrive(len(cuts) + 2 * at + 1)
+        part = mm(both_ref[2 * low : 2 * high, :], w_ref[2 * low : 2 * high, :], TN)
+        if at > 0:
+            part = acc_ref[...] + part
+        if at < len(cuts) - 1:
+            acc_ref[...] = part
         else:
-            there = slice(cols.start - half, cols.stop - half)
-            late = mm(back_ref[...], part, NN).astype(jnp.bfloat16)
-            keepb_ref[:, there] = late[:kept]
-            sendb_ref[:, there] = late[kept:]
+            first = part[:, :half].astype(jnp.bfloat16)
+            keepa_ref[...] = first[:kept]
+            senda_ref[...] = first[kept:]
+            late = mm(back_ref[...], part[:, half:].astype(jnp.bfloat16), NN).astype(jnp.bfloat16)
+            keepb_ref[...] = late[:kept]
+            sendb_ref[...] = late[kept:]
 
 
 def signal_call(perm, back, parts, pg, pu, wg, wu, wd):
     inner, width = wg.shape
     rows = perm.shape[0]
-    cuts = cuts_of(inner, 256)
-    grant = (63 << 20) - 2 * wg.size - (SPARE_MIB << 20)
+    cuts = cuts_of(inner, STEP)
+    vmem = pl.BlockSpec(memory_space=pltpu.VMEM)
+    hbm = pl.BlockSpec(memory_space=pl.ANY)
     return pl.pallas_call(
         functools.partial(signal_kernel, cuts),
-        in_specs=[VMEM] * 9 + [ANY] * 2,
-        out_specs=[VMEM] * 8,
+        in_specs=[vmem] * 8 + [hbm] * 3,
+        out_specs=[vmem] * 8,
         out_shape=[jax.ShapeDtypeStruct((rows, width), jnp.bfloat16)]
         + [jax.ShapeDtypeStruct((inner, rows), jnp.bfloat16)] * 3
         + [jax.ShapeDtypeStruct((rows // 2, width // 2), jnp.bfloat16)] * 4,
         scratch_shapes=[
+            pltpu.VMEM((2 * inner, rows), jnp.bfloat16),
+            pltpu.VMEM((2 * inner, width), jnp.bfloat16),
+            pltpu.VMEM((inner, width), jnp.bfloat16),
             pltpu.VMEM((rows, width), jnp.float32),
-            pltpu.VMEM((inner, width), jnp.bfloat16),
-            pltpu.VMEM((inner, width), jnp.bfloat16),
-            pltpu.SemaphoreType.DMA((2, len(cuts))),
+            pltpu.SemaphoreType.DMA((3, len(cuts))),
         ],
-        compiler_params=pltpu.CompilerParams(vmem_limit_bytes=grant),
+        compiler_params=pltpu.CompilerParams(vmem_limit_bytes=SIGNAL_MIB << 20),
         cost_estimate=pl.CostEstimate(
             flops=6 * inner * width * rows, bytes_accessed=6 * inner * width, transcendentals=inner * rows
         ),
@@ -317,11 +330,10 @@
         held_s = grow(held_s, got_s)
         got_s = send(held_s, stage)
     held_s = grow(held_s, got_s)
-    wg, wu_here = loaded
-    held_t, got_t, held_s, wg, wu_here = tie((held_t, got_t, held_s, wg, wu_here))
+    held_t, got_t, held_s, wg_here, wu_here = tie((held_t, got_t, held_s, *loaded))
     parts_t = (held_t[0], got_t[0], held_t[1], got_t[1])
     got_s = send(held_s, bits - 2)
-    t, pg = gate_call(perm, parts_t, wg)
+    t, pg = gate_call(perm, parts_t, wg_here)
     held_s = grow(held_s, got_s)
     t, pg, held_s = tie((t, pg, held_s))
     got_s = send(held_s, bits - 1)
@@ -335,8 +347,9 @@
     kept, sent = (keepa, keepb), (senda, sendb)
     for at, stage in enumerate(range(bits - 1, -1, -1)):
         got = send(sent, stage)
-        if at < len(work):
-            grads.append(weight_call(*work[at]))
+        for _ in range(2 if at == 0 else 1):
+            if len(grads) < len(work):
+                grads.append(weight_call(*work[len(grads)]))
         sums = tuple((x.astype(jnp.float32) + y.astype(jnp.float32)).astype(jnp.bfloat16) for x, y in zip(kept, got))
         sums, grads, work = tie((sums, grads, work))
         kept = tuple(x[: x.shape[0] // 2] for x in sums)

time: 116 us -> 112 us (0.966)
  Pallas kernels: 48.2 us -> 44.2 us
  waiting for transfers between devices: 28.9 us -> 27 us
  starting transfers between devices: 30.6 us -> 31.9 us
    pallas_call x1, Pallas kernels: 18.3 us -> 14.4 us  [signal_call(): pl.pallas_call(functools.partial(signal_kernel, cuts), in_specs=[vmem] *...]
    ppermute x27, waiting for transfers between devices: 28.9 us -> 27 us  [swap(): lax.ppermute(value, axis, [(i, i ^ offset) for i in range(size)])[:rows]]
    ppermute x27, starting transfers between devices: 30.6 us -> 31.9 us  [swap(): lax.ppermute(value, axis, [(i, i ^ offset) for i in range(size)])[:rows]]
  transfers between devices with their start and end apart: 27 -> 27, of which waited for: 17 -> 17; matrix products, arithmetic and copies ran while one was open for 3% -> 3% of each run, Pallas kernels for 26% -> 27%
where the time goes in v3:
time: 112 us
  Pallas kernels  44.2 us (39%)
  starting transfers between devices  31.9 us (28%)
  waiting for transfers between devices  27 us (24%)
  matrix products  3.38 us (3%)
  other arithmetic  2.87 us (3%)
  between operations  1.86 us (2%)
    ppermute x27, starting transfers between devices, swap(): lax.ppermute(value, axis, [(i, i ^ offset) for i in range(size)])[:rows]  31.9 us
    ppermute x27, waiting for transfers between devices, swap(): lax.ppermute(value, axis, [(i, i ^ offset) for i in range(size)])[:rows]  27 us
    pallas_call x3, Pallas kernels, weight_call(): pl.pallas_call(functools.partial(weight_kernel, cuts), in_specs=[pl.Block...  14.9 us
    pallas_call x1, Pallas kernels, signal_call(): pl.pallas_call(functools.partial(signal_kernel, cuts), in_specs=[vmem] *...  14.4 us
    pallas_call x2, Pallas kernels, load_call(): pl.pallas_call(functools.partial(load_kernel, cuts), in_specs=[pl.BlockSp...  8.64 us
    pallas_call x1, Pallas kernels, gate_call(): pl.pallas_call(functools.partial(gate_kernel, cuts_of(inner, STEP)), in_s...  3.22 us
    pallas_call x1, Pallas kernels, up_call(): pl.pallas_call(functools.partial(up_kernel, cuts_of(inner, STEP)), in_spe...  3.08 us
  transfers between devices with their start and end apart: 27, of which 17 were waited for; matrix products, arithmetic and copies ran while one was open for 3% of the time, Pallas kernels for 27%

profile of v3, /device:TPU:0, one launch (start us, length us, event | category | flops | bytes accessed | tf_op | source)
XLA Modules:
  0.0 111.8 jit_solution(9819218149732522161)
XLA Ops:
  3.6 2.6 %collective-permute-start.1 = (bf16[8,4096]{1,0:T(8,128)(2,1)S(1)}, bf16[8,4096]{1,0:T(8,128)(2,1)S(1)}, u32[]{:S(2)}, u32[]{:S(2)}) collective-permute-start(bf16[8,4096]{1,0:T(8,128)(2,1)S(1)} %concatenate.79), channel_id=1, source_target_pairs={{0,16},{8,24},{16,0},{24,8},{1,17},{9,25},{17,1},{25,9},{2,18},{10... | collective-permute-start | bytes 196616 | tf_op jit(solution)/shard_map/ppermute | solution.py:270
  9.0 2.0 %collective-permute-start.8 = (bf16[8,4096]{1,0:T(8,128)(2,1)S(1)}, bf16[8,4096]{1,0:T(8,128)(2,1)S(1)}, u32[]{:S(2)}, u32[]{:S(2)}) collective-permute-start(bf16[8,4096]{1,0:T(8,128)(2,1)S(1)} %concatenate.89), channel_id=1, source_target_pairs={{0,16},{8,24},{16,0},{24,8},{1,17},{9,25},{17,1},{25,9},{2,18},{10... | collective-permute-start | bytes 196616 | tf_op jit(solution)/shard_map/ppermute | solution.py:270
  13.0 2.6 %collective-permute-start.3 = (bf16[24,2048]{1,0:T(8,128)(2,1)S(1)}, bf16[24,2048]{1,0:T(8,128)(2,1)S(1)}, u32[]{:S(2)}, u32[]{:S(2)}) collective-permute-start(bf16[24,2048]{1,0:T(8,128)(2,1)S(1)} %concatenate.82), channel_id=1, source_target_pairs={{0,4},{1,5},{2,6},{3,7},{4,0},{5,1},{6,2},{7,3},{8,12},{9,13},{10,... | collective-permute-start | bytes 294920 | tf_op jit(solution)/shard_map/ppermute | solution.py:270
  15.7 4.3 %shard_map.129.wg_ref = bf16[1376,4096]{1,0:T(8,128)(2,1)S(1)} custom-call(bf16[1376,4096]{1,0:T(8,128)(2,1)} %bitcast.62), custom_call_target="tpu_custom_call" | custom-call | bytes 11272192 | tf_op jit(solution)/shard_map/pallas_call | solution.py:89
  21.8 3.4 %collective-permute-start.6 = (bf16[40,2048]{1,0:T(8,128)(2,1)S(1)}, bf16[40,2048]{1,0:T(8,128)(2,1)S(1)}, u32[]{:S(2)}, u32[]{:S(2)}) collective-permute-start(bf16[40,2048]{1,0:T(8,128)(2,1)S(1)} %pad_maximum_fusion.7), channel_id=1, source_target_pairs={{0,4},{1,5},{2,6},{3,7},{4,0},{5,1},{6,2},{7,3},{8,12},{9,13},{10,... | collective-permute-start | bytes 491528 | tf_op jit(solution)/shard_map/ppermute | solution.py:270
  25.2 4.3 %shard_map.130.wu_ref = bf16[1376,4096]{1,0:T(8,128)(2,1)S(1)} custom-call(bf16[1376,4096]{1,0:T(8,128)(2,1)} %bitcast.64), custom_call_target="tpu_custom_call" | custom-call | bytes 11272192 | tf_op jit(solution)/shard_map/pallas_call | solution.py:89
  29.8 3.1 %collective-permute-done.6 = bf16[40,2048]{1,0:T(8,128)(2,1)S(1)} collective-permute-done((bf16[40,2048]{1,0:T(8,128)(2,1)S(1)}, bf16[40,2048]{1,0:T(8,128)(2,1)S(1)}, u32[]{:S(2)}, u32[]{:S(2)}) %collective-permute-start.6) | collective-permute-done | bytes 163872 | tf_op jit(solution)/shard_map/ppermute | solution.py:270
  35.2 2.9 %collective-permute-start.11 = (bf16[80,2048]{1,0:T(8,128)(2,1)S(1)}, bf16[80,2048]{1,0:T(8,128)(2,1)S(1)}, u32[]{:S(2)}, u32[]{:S(2)}) collective-permute-start(bf16[80,2048]{1,0:T(8,128)(2,1)S(1)} %pad_maximum_fusion.1.b0_ref), channel_id=1, source_target_pairs={{0,2},{1,3},{2,0},{3,1},{4,6},{5,7},{6,4},{7,5},{8,10},{9,11},{10,... | collective-permute-start | bytes 983048 | tf_op jit(solution)/shard_map/ppermute | solution.py:270
  38.7 1.8 %collective-permute-done.12 = bf16[24,2048]{1,0:T(8,128)(2,1)S(1)} collective-permute-done((bf16[24,2048]{1,0:T(8,128)(2,1)S(1)}, bf16[24,2048]{1,0:T(8,128)(2,1)S(1)}, u32[]{:S(2)}, u32[]{:S(2)}) %collective-permute-start.12) | collective-permute-done | bytes 98336 | tf_op jit(solution)/shard_map/ppermute | solution.py:270
  40.5 3.0 %collective-permute-done.10.a1_ref = bf16[80,2048]{1,0:T(8,128)(2,1)S(1)} collective-permute-done((bf16[80,2048]{1,0:T(8,128)(2,1)S(1)}, bf16[80,2048]{1,0:T(8,128)(2,1)S(1)}, u32[]{:S(2)}, u32[]{:S(2)}) %collective-permute-start.10) | collective-permute-done | bytes 327712 | tf_op jit(solution)/shard_map/ppermute | solution.py:270
  43.6 1.8 %collective-permute-done.11.b1_ref = bf16[80,2048]{1,0:T(8,128)(2,1)S(1)} collective-permute-done((bf16[80,2048]{1,0:T(8,128)(2,1)S(1)}, bf16[80,2048]{1,0:T(8,128)(2,1)S(1)}, u32[]{:S(2)}, u32[]{:S(2)}) %collective-permute-start.11) | collective-permute-done | bytes 327712 | tf_op jit(solution)/shard_map/ppermute | solution.py:270
  46.0 2.4 %collective-permute-start.15 = (bf16[40,2048]{1,0:T(8,128)(2,1)S(1)}, bf16[40,2048]{1,0:T(8,128)(2,1)S(1)}, u32[]{:S(2)}, u32[]{:S(2)}) collective-permute-start(bf16[40,2048]{1,0:T(8,128)(2,1)S(1)} %pad_maximum_fusion.9), channel_id=1, source_target_pairs={{0,4},{1,5},{2,6},{3,7},{4,0},{5,1},{6,2},{7,3},{8,12},{9,13},{10,... | collective-permute-start | bytes 491528 | tf_op jit(solution)/shard_map/ppermute | solution.py:270
  48.4 3.2 %shard_map.131 = (bf16[160,4096]{1,0:T(8,128)(2,1)S(1)}, f32[1376,160]{1,0:T(8,128)S(1)}) custom-call(bf16[160,160]{1,0:T(8,128)(2,1)S(1)} %copy-done.2, bf16[80,2048]{1,0:T(8,128)(2,1)S(1)} %pad_maximum_fusion.a0_ref, bf16[80,2048]{1,0:T(8,128)(2,1)S(1)} %collective-permute-done.10.a1_ref, bf16[80,2048]{1,0:T(8,128)(2,1)S(1)} %pad_maximum_fusion.1.b0_ref, ...), custom_call_target="tpu_custom_call" | custom-call | flops 1803550720 | bytes 11272192 | tf_op jit(solution)/shard_map/pallas_call | solution.py:110
  52.7 2.6 %collective-permute-done.15 = bf16[40,2048]{1,0:T(8,128)(2,1)S(1)} collective-permute-done((bf16[40,2048]{1,0:T(8,128)(2,1)S(1)}, bf16[40,2048]{1,0:T(8,128)(2,1)S(1)}, u32[]{:S(2)}, u32[]{:S(2)}) %collective-permute-start.15) | collective-permute-done | bytes 163872 | tf_op jit(solution)/shard_map/ppermute | solution.py:270
  56.2 3.1 %shard_map.132.pu_ref = f32[1376,160]{1,0:T(8,128)S(1)} custom-call(bf16[160,4096]{1,0:T(8,128)(2,1)S(1)} %get-tuple-element.110.t_ref.x_ref, bf16[1376,4096]{1,0:T(8,128)(2,1)S(1)} %shard_map.130.wu_ref), custom_call_target="tpu_custom_call" | custom-call | flops 1803550720 | bytes 11272192 | tf_op jit(solution)/shard_map/pallas_call | solution.py:134
  59.2 3.3 %collective-permute-done.16.a1_ref = bf16[80,2048]{1,0:T(8,128)(2,1)S(1)} collective-permute-done((bf16[80,2048]{1,0:T(8,128)(2,1)S(1)}, bf16[80,2048]{1,0:T(8,128)(2,1)S(1)}, u32[]{:S(2)}, u32[]{:S(2)}) %collective-permute-start.16) | collective-permute-done | bytes 327712 | tf_op jit(solution)/shard_map/ppermute | solution.py:270
  63.2 14.4 %shard_map.133 = (bf16[160,4096]{1,0:T(8,128)(2,1)S(1)}, bf16[1376,160]{1,0:T(8,128)(2,1)S(1)}, bf16[1376,160]{1,0:T(8,128)(2,1)S(1)}, bf16[1376,160]{1,0:T(8,12...) custom-call(bf16[160,160]{1,0:T(8,128)(2,1)S(1)} %copy-done.2, ...), custom_call_target="tpu_custom_call" | custom-call | flops 5410652160 | bytes 33816576 | tf_op jit(solution)/shard_map/pallas_call | solution.py:209
  79.6 5.0 %shard_map.135 = bf16[1376,4096]{1,0:T(8,128)(2,1)} custom-call(bf16[160,4096]{1,0:T(8,128)(2,1)S(1)} %get-tuple-element.110.t_ref.x_ref, bf16[1376,160]{1,0:T(8,128)(2,1)S(1)} %get-tuple-element.104.g_ref), custom_call_target="tpu_custom_call" | custom-call | flops 1803550720 | bytes 11272192 | tf_op jit(solution)/shard_map/pallas_call | solution.py:252
  84.6 5.0 %shard_map.134 = bf16[1376,4096]{1,0:T(8,128)(2,1)} custom-call(bf16[160,4096]{1,0:T(8,128)(2,1)S(1)} %get-tuple-element.102.x_ref, bf16[1376,160]{1,0:T(8,128)(2,1)S(1)} %get-tuple-element.103.g_ref), custom_call_target="tpu_custom_call" | custom-call | flops 1803550720 | bytes 11272192 | tf_op jit(solution)/shard_map/pallas_call | solution.py:252
  89.8 2.1 %collective-permute-start.21 = (bf16[40,2048]{1,0:T(8,128)(2,1)S(1)}, bf16[40,2048]{1,0:T(8,128)(2,1)S(1)}, u32[]{:S(2)}, u32[]{:S(2)}) collective-permute-start(bf16[40,2048]{1,0:T(8,128)(2,1)S(1)} %slice.148), channel_id=1, source_target_pairs={{0,4},{1,5},{2,6},{3,7},{4,0},{5,1},{6,2},{7,3},{8,12},{9,13},{10,... | collective-permute-start | bytes 491528 | tf_op jit(solution)/shard_map/ppermute | solution.py:270
  92.5 5.0 %shard_map.136 = bf16[1376,4096]{1,0:T(8,128)(2,1)} custom-call(bf16[160,4096]{1,0:T(8,128)(2,1)S(1)} %get-tuple-element.110.t_ref.x_ref, bf16[1376,160]{1,0:T(8,128)(2,1)S(1)} %get-tuple-element.111.g_ref), custom_call_target="tpu_custom_call" | custom-call | flops 1803550720 | bytes 11272192 | tf_op jit(solution)/shard_map/pallas_call | solution.py:252
  98.7 1.9 %collective-permute-start.22 = (bf16[24,2048]{1,0:T(8,128)(2,1)S(1)}, bf16[24,2048]{1,0:T(8,128)(2,1)S(1)}, u32[]{:S(2)}, u32[]{:S(2)}) collective-permute-start(bf16[24,2048]{1,0:T(8,128)(2,1)S(1)} %concatenate.98), channel_id=1, source_target_pairs={{0,4},{1,5},{2,6},{3,7},{4,0},{5,1},{6,2},{7,3},{8,12},{9,13},{10,... | collective-permute-start | bytes 294920 | tf_op jit(solution)/shard_map/ppermute | solution.py:270
  100.6 2.3 %collective-permute-done.23 = bf16[24,2048]{1,0:T(8,128)(2,1)S(1)} collective-permute-done((bf16[24,2048]{1,0:T(8,128)(2,1)S(1)}, bf16[24,2048]{1,0:T(8,128)(2,1)S(1)}, u32[]{:S(2)}, u32[]{:S(2)}) %collective-permute-start.23) | collective-permute-done | bytes 98336 | tf_op jit(solution)/shard_map/ppermute | solution.py:270
  106.5 2.6 %collective-permute-done.25 = bf16[8,4096]{1,0:T(8,128)(2,1)S(1)} collective-permute-done((bf16[8,4096]{1,0:T(8,128)(2,1)S(1)}, bf16[8,4096]{1,0:T(8,128)(2,1)S(1)}, u32[]{:S(2)}, u32[]{:S(2)}) %collective-permute-start.25) | collective-permute-done | bytes 65568 | tf_op jit(solution)/shard_map/ppermute | solution.py:270
  (105 shorter events, 25.4 us)
Async XLA Ops:
  3.0 8.1 %collective-permute-start = (bf16[8,4096]{1,0:T(8,128)(2,1)S(1)}, bf16[8,4096]{1,0:T(8,128)(2,1)S(1)}, u32[]{:S(2)}, u32[]{:S(2)}) collective-permute-start(bf16[8,4096]{1,0:T(8,128)(2,1)S(1)} %concatenate.78), channel_id=1, source_target_pairs={{0,8},{8,0},{16,24},{24,16},{1,9},{9,1},{17,25},{25,17},{2,10},{10... | collective-permute-start | bytes 196616 | tf_op jit(solution)/shard_map/ppermute | solution.py:270
  3.6 7.6 %collective-permute-start.1 = (bf16[8,4096]{1,0:T(8,128)(2,1)S(1)}, bf16[8,4096]{1,0:T(8,128)(2,1)S(1)}, u32[]{:S(2)}, u32[]{:S(2)}) collective-permute-start(bf16[8,4096]{1,0:T(8,128)(2,1)S(1)} %concatenate.79), channel_id=1, source_target_pairs={{0,16},{8,24},{16,0},{24,8},{1,17},{9,25},{17,1},{25,9},{2,18},{10... | collective-permute-start | bytes 196616 | tf_op jit(solution)/shard_map/ppermute | solution.py:270
  6.1 5.0 %collective-permute-start.2 = (bf16[8,4096]{1,0:T(8,128)(2,1)S(1)}, bf16[8,4096]{1,0:T(8,128)(2,1)S(1)}, u32[]{:S(2)}, u32[]{:S(2)}) collective-permute-start(bf16[8,4096]{1,0:T(8,128)(2,1)S(1)} %concatenate.80), channel_id=1, source_target_pairs={{0,24},{8,16},{16,8},{24,0},{1,25},{9,17},{17,9},{25,1},{2,26},{10... | collective-permute-start | bytes 196616 | tf_op jit(solution)/shard_map/ppermute | solution.py:270
  8.8 6.7 %collective-permute-start.7 = (bf16[8,4096]{1,0:T(8,128)(2,1)S(1)}, bf16[8,4096]{1,0:T(8,128)(2,1)S(1)}, u32[]{:S(2)}, u32[]{:S(2)}) collective-permute-start(bf16[8,4096]{1,0:T(8,128)(2,1)S(1)} %concatenate.88), channel_id=1, source_target_pairs={{0,8},{8,0},{16,24},{24,16},{1,9},{9,1},{17,25},{25,17},{2,10},{10... | collective-permute-start | bytes 196616 | tf_op jit(solution)/shard_map/ppermute | solution.py:270
  9.0 6.5 %collective-permute-start.8 = (bf16[8,4096]{1,0:T(8,128)(2,1)S(1)}, bf16[8,4096]{1,0:T(8,128)(2,1)S(1)}, u32[]{:S(2)}, u32[]{:S(2)}) collective-permute-start(bf16[8,4096]{1,0:T(8,128)(2,1)S(1)} %concatenate.89), channel_id=1, source_target_pairs={{0,16},{8,24},{16,0},{24,8},{1,17},{9,25},{17,1},{25,9},{2,18},{10... | collective-permute-start | bytes 196616 | tf_op jit(solution)/shard_map/ppermute | solution.py:270
  11.3 8.7 %collective-permute-start.4 = (bf16[24,2048]{1,0:T(8,128)(2,1)S(1)}, bf16[24,2048]{1,0:T(8,128)(2,1)S(1)}, u32[]{:S(2)}, u32[]{:S(2)}) collective-permute-start(bf16[24,2048]{1,0:T(8,128)(2,1)S(1)} %concatenate.84), channel_id=1, source_target_pairs={{0,1},{1,0},{2,3},{3,2},{4,5},{5,4},{6,7},{7,6},{8,9},{9,8},{10,11... | collective-permute-start | bytes 294920 | tf_op jit(solution)/shard_map/ppermute | solution.py:270
  13.0 8.0 %collective-permute-start.3 = (bf16[24,2048]{1,0:T(8,128)(2,1)S(1)}, bf16[24,2048]{1,0:T(8,128)(2,1)S(1)}, u32[]{:S(2)}, u32[]{:S(2)}) collective-permute-start(bf16[24,2048]{1,0:T(8,128)(2,1)S(1)} %concatenate.82), channel_id=1, source_target_pairs={{0,4},{1,5},{2,6},{3,7},{4,0},{5,1},{6,2},{7,3},{8,12},{9,13},{10,... | collective-permute-start | bytes 294920 | tf_op jit(solution)/shard_map/ppermute | solution.py:270
  21.0 8.8 %collective-permute-start.5 = (bf16[40,2048]{1,0:T(8,128)(2,1)S(1)}, bf16[40,2048]{1,0:T(8,128)(2,1)S(1)}, u32[]{:S(2)}, u32[]{:S(2)}) collective-permute-start(bf16[40,2048]{1,0:T(8,128)(2,1)S(1)} %pad_maximum_fusion.6), channel_id=1, source_target_pairs={{0,2},{1,3},{2,0},{3,1},{4,6},{5,7},{6,4},{7,5},{8,10},{9,11},{10,... | collective-permute-start | bytes 491528 | tf_op jit(solution)/shard_map/ppermute | solution.py:270
  21.8 11.1 %collective-permute-start.6 = (bf16[40,2048]{1,0:T(8,128)(2,1)S(1)}, bf16[40,2048]{1,0:T(8,128)(2,1)S(1)}, u32[]{:S(2)}, u32[]{:S(2)}) collective-permute-start(bf16[40,2048]{1,0:T(8,128)(2,1)S(1)} %pad_maximum_fusion.7), channel_id=1, source_target_pairs={{0,4},{1,5},{2,6},{3,7},{4,0},{5,1},{6,2},{7,3},{8,12},{9,13},{10,... | collective-permute-start | bytes 491528 | tf_op jit(solution)/shard_map/ppermute | solution.py:270
  32.9 5.7 %collective-permute-start.13 = (bf16[24,2048]{1,0:T(8,128)(2,1)S(1)}, bf16[24,2048]{1,0:T(8,128)(2,1)S(1)}, u32[]{:S(2)}, u32[]{:S(2)}) collective-permute-start(bf16[24,2048]{1,0:T(8,128)(2,1)S(1)} %concatenate.94), channel_id=1, source_target_pairs={{0,1},{1,0},{2,3},{3,2},{4,5},{5,4},{6,7},{7,6},{8,9},{9,8},{10,11... | collective-permute-start | bytes 294920 | tf_op jit(solution)/shard_map/ppermute | solution.py:270
  33.8 6.6 %collective-permute-start.12 = (bf16[24,2048]{1,0:T(8,128)(2,1)S(1)}, bf16[24,2048]{1,0:T(8,128)(2,1)S(1)}, u32[]{:S(2)}, u32[]{:S(2)}) collective-permute-start(bf16[24,2048]{1,0:T(8,128)(2,1)S(1)} %concatenate.92), channel_id=1, source_target_pairs={{0,4},{1,5},{2,6},{3,7},{4,0},{5,1},{6,2},{7,3},{8,12},{9,13},{10,... | collective-permute-start | bytes 294920 | tf_op jit(solution)/shard_map/ppermute | solution.py:270
  34.1 9.4 %collective-permute-start.10 = (bf16[80,2048]{1,0:T(8,128)(2,1)S(1)}, bf16[80,2048]{1,0:T(8,128)(2,1)S(1)}, u32[]{:S(2)}, u32[]{:S(2)}) collective-permute-start(bf16[80,2048]{1,0:T(8,128)(2,1)S(1)} %pad_maximum_fusion.a0_ref), channel_id=1, source_target_pairs={{0,1},{1,0},{2,3},{3,2},{4,5},{5,4},{6,7},{7,6},{8,9},{9,8},{10,11... | collective-permute-start | bytes 983048 | tf_op jit(solution)/shard_map/ppermute | solution.py:270
  35.2 10.1 %collective-permute-start.11 = (bf16[80,2048]{1,0:T(8,128)(2,1)S(1)}, bf16[80,2048]{1,0:T(8,128)(2,1)S(1)}, u32[]{:S(2)}, u32[]{:S(2)}) collective-permute-start(bf16[80,2048]{1,0:T(8,128)(2,1)S(1)} %pad_maximum_fusion.1.b0_ref), channel_id=1, source_target_pairs={{0,2},{1,3},{2,0},{3,1},{4,6},{5,7},{6,4},{7,5},{8,10},{9,11},{10,... | collective-permute-start | bytes 983048 | tf_op jit(solution)/shard_map/ppermute | solution.py:270
  45.3 7.3 %collective-permute-start.14 = (bf16[40,2048]{1,0:T(8,128)(2,1)S(1)}, bf16[40,2048]{1,0:T(8,128)(2,1)S(1)}, u32[]{:S(2)}, u32[]{:S(2)}) collective-permute-start(bf16[40,2048]{1,0:T(8,128)(2,1)S(1)} %pad_maximum_fusion.8), channel_id=1, source_target_pairs={{0,2},{1,3},{2,0},{3,1},{4,6},{5,7},{6,4},{7,5},{8,10},{9,11},{10,... | collective-permute-start | bytes 491528 | tf_op jit(solution)/shard_map/ppermute | solution.py:270
  46.0 9.3 %collective-permute-start.15 = (bf16[40,2048]{1,0:T(8,128)(2,1)S(1)}, bf16[40,2048]{1,0:T(8,128)(2,1)S(1)}, u32[]{:S(2)}, u32[]{:S(2)}) collective-permute-start(bf16[40,2048]{1,0:T(8,128)(2,1)S(1)} %pad_maximum_fusion.9), channel_id=1, source_target_pairs={{0,4},{1,5},{2,6},{3,7},{4,0},{5,1},{6,2},{7,3},{8,12},{9,13},{10,... | collective-permute-start | bytes 491528 | tf_op jit(solution)/shard_map/ppermute | solution.py:270
  55.4 7.1 %collective-permute-start.16 = (bf16[80,2048]{1,0:T(8,128)(2,1)S(1)}, bf16[80,2048]{1,0:T(8,128)(2,1)S(1)}, u32[]{:S(2)}, u32[]{:S(2)}) collective-permute-start(bf16[80,2048]{1,0:T(8,128)(2,1)S(1)} %pad_maximum_fusion.2.a0_ref), channel_id=1, source_target_pairs={{0,1},{1,0},{2,3},{3,2},{4,5},{5,4},{6,7},{7,6},{8,9},{9,8},{10,11... | collective-permute-start | bytes 983048 | tf_op jit(solution)/shard_map/ppermute | solution.py:270
  56.1 7.1 %collective-permute-start.17 = (bf16[80,2048]{1,0:T(8,128)(2,1)S(1)}, bf16[80,2048]{1,0:T(8,128)(2,1)S(1)}, u32[]{:S(2)}, u32[]{:S(2)}) collective-permute-start(bf16[80,2048]{1,0:T(8,128)(2,1)S(1)} %pad_maximum_fusion.3.b0_ref), channel_id=1, source_target_pairs={{0,2},{1,3},{2,0},{3,1},{4,6},{5,7},{6,4},{7,5},{8,10},{9,11},{10,... | collective-permute-start | bytes 983048 | tf_op jit(solution)/shard_map/ppermute | solution.py:270
  77.6 11.9 %collective-permute-start.18 = (bf16[80,2048]{1,0:T(8,128)(2,1)S(1)}, bf16[80,2048]{1,0:T(8,128)(2,1)S(1)}, u32[]{:S(2)}, u32[]{:S(2)}) collective-permute-start(bf16[80,2048]{1,0:T(8,128)(2,1)S(1)} %get-tuple-element.99), channel_id=1, source_target_pairs={{0,1},{1,0},{2,3},{3,2},{4,5},{5,4},{6,7},{7,6},{8,9},{9,8},{10,11... | collective-permute-start | bytes 983048 | tf_op jit(solution)/shard_map/ppermute | solution.py:270
  79.0 10.6 %collective-permute-start.19 = (bf16[80,2048]{1,0:T(8,128)(2,1)S(1)}, bf16[80,2048]{1,0:T(8,128)(2,1)S(1)}, u32[]{:S(2)}, u32[]{:S(2)}) collective-permute-start(bf16[80,2048]{1,0:T(8,128)(2,1)S(1)} %get-tuple-element.101), channel_id=1, source_target_pairs={{0,2},{1,3},{2,0},{3,1},{4,6},{5,7},{6,4},{7,5},{8,10},{9,11},{10,... | collective-permute-start | bytes 983048 | tf_op jit(solution)/shard_map/ppermute | solution.py:270
  89.8 8.1 %collective-permute-start.21 = (bf16[40,2048]{1,0:T(8,128)(2,1)S(1)}, bf16[40,2048]{1,0:T(8,128)(2,1)S(1)}, u32[]{:S(2)}, u32[]{:S(2)}) collective-permute-start(bf16[40,2048]{1,0:T(8,128)(2,1)S(1)} %slice.148), channel_id=1, source_target_pairs={{0,4},{1,5},{2,6},{3,7},{4,0},{5,1},{6,2},{7,3},{8,12},{9,13},{10,... | collective-permute-start | bytes 491528 | tf_op jit(solution)/shard_map/ppermute | solution.py:270
  91.9 6.2 %collective-permute-start.20 = (bf16[40,2048]{1,0:T(8,128)(2,1)S(1)}, bf16[40,2048]{1,0:T(8,128)(2,1)S(1)}, u32[]{:S(2)}, u32[]{:S(2)}) collective-permute-start(bf16[40,2048]{1,0:T(8,128)(2,1)S(1)} %slice.146), channel_id=1, source_target_pairs={{0,2},{1,3},{2,0},{3,1},{4,6},{5,7},{6,4},{7,5},{8,10},{9,11},{10,... | collective-permute-start | bytes 491528 | tf_op jit(solution)/shard_map/ppermute | solution.py:270
  98.2 4.7 %collective-permute-start.23 = (bf16[24,2048]{1,0:T(8,128)(2,1)S(1)}, bf16[24,2048]{1,0:T(8,128)(2,1)S(1)}, u32[]{:S(2)}, u32[]{:S(2)}) collective-permute-start(bf16[24,2048]{1,0:T(8,128)(2,1)S(1)} %concatenate.99), channel_id=1, source_target_pairs={{0,1},{1,0},{2,3},{3,2},{4,5},{5,4},{6,7},{7,6},{8,9},{9,8},{10,11... | collective-permute-start | bytes 294920 | tf_op jit(solution)/shard_map/ppermute | solution.py:270
  98.7 5.6 %collective-permute-start.22 = (bf16[24,2048]{1,0:T(8,128)(2,1)S(1)}, bf16[24,2048]{1,0:T(8,128)(2,1)S(1)}, u32[]{:S(2)}, u32[]{:S(2)}) collective-permute-start(bf16[24,2048]{1,0:T(8,128)(2,1)S(1)} %concatenate.98), channel_id=1, source_target_pairs={{0,4},{1,5},{2,6},{3,7},{4,0},{5,1},{6,2},{7,3},{8,12},{9,13},{10,... | collective-permute-start | bytes 294920 | tf_op jit(solution)/shard_map/ppermute | solution.py:270
  104.5 4.6 %collective-permute-start.25 = (bf16[8,4096]{1,0:T(8,128)(2,1)S(1)}, bf16[8,4096]{1,0:T(8,128)(2,1)S(1)}, u32[]{:S(2)}, u32[]{:S(2)}) collective-permute-start(bf16[8,4096]{1,0:T(8,128)(2,1)S(1)} %concatenate.102), channel_id=1, source_target_pairs={{0,16},{8,24},{16,0},{24,8},{1,17},{9,25},{17,1},{25,9},{2,18},{10... | collective-permute-start | bytes 196616 | tf_op jit(solution)/shard_map/ppermute | solution.py:270
  (7 other events, 84.1 us)

commit v4 on v3

--- a/solution.py
+++ b/solution.py
@@ -13,7 +13,7 @@
 SLOTS = 3
 STEP = 512
 AHEAD = 4
-SIGNAL_MIB = 44
+SIGNAL_MIB = 28
 SMALL_MIB = 12
 
 NT = (((1,), (1,)), ((), ()))
@@ -144,18 +144,15 @@
 
 
 def signal_kernel(
-    cuts, perm_ref, back_ref, a0_ref, a1_ref, b0_ref, b1_ref, pg_ref, pu_ref, wg_hbm, wu_hbm, wd_hbm,
-    s_ref, h_ref, gs_ref, us_ref, keepa_ref, senda_ref, keepb_ref, sendb_ref, both_ref, w_ref, wd_ref, acc_ref, sems,
+    cuts, perm_ref, back_ref, a0_ref, a1_ref, b0_ref, b1_ref, pg_ref, pu_ref, wd_ref, wg_hbm, wu_hbm,
+    s_ref, h_ref, gs_ref, us_ref, keepa_ref, senda_ref, keepb_ref, sendb_ref, both_ref, w_ref, acc_ref, sems,
 ):
     copies = []
-    for at, (low, high) in enumerate(cuts):
-        rows = pl.ds(low, high - low)
-        copies.append(pltpu.make_async_copy(wd_hbm.at[rows, :], wd_ref.at[rows, :], sems.at[0, at]))
     for at, (low, high) in enumerate(cuts):
         size = high - low
         for side, src in enumerate((wg_hbm, wu_hbm)):
             dst = w_ref.at[pl.ds(2 * low + side * size, size), :]
-            copies.append(pltpu.make_async_copy(src.at[pl.ds(low, size), :], dst, sems.at[1 + side, at]))
+            copies.append(pltpu.make_async_copy(src.at[pl.ds(low, size), :], dst, sems.at[side, at]))
     for copy in copies[:AHEAD]:
         copy.start()
 
@@ -173,7 +170,6 @@
         logistic = jax.nn.sigmoid(gate)
         swished = gate * logistic
         h_ref[low:high, :] = (swished * up).astype(jnp.bfloat16)
-        arrive(at)
         hidden_grad = mm(wd_ref[low:high, :], s, NT)
         gs = (hidden_grad * up * logistic * (1.0 + gate * (1.0 - logistic))).astype(jnp.bfloat16)
         us = (hidden_grad * swished).astype(jnp.bfloat16)
@@ -184,8 +180,8 @@
     half = keepa_ref.shape[1]
     kept = keepa_ref.shape[0]
     for at, (low, high) in enumerate(cuts):
-        arrive(len(cuts) + 2 * at)
-        arrive(len(cuts) + 2 * at + 1)
+        arrive(2 * at)
+        arrive(2 * at + 1)
         part = mm(both_ref[2 * low : 2 * high, :], w_ref[2 * low : 2 * high, :], TN)
         if at > 0:
             part = acc_ref[...] + part
@@ -208,7 +204,7 @@
     hbm = pl.BlockSpec(memory_space=pl.ANY)
     return pl.pallas_call(
         functools.partial(signal_kernel, cuts),
-        in_specs=[vmem] * 8 + [hbm] * 3,
+        in_specs=[vmem] * 9 + [hbm] * 2,
         out_specs=[vmem] * 8,
         out_shape=[jax.ShapeDtypeStruct((rows, width), jnp.bfloat16)]
         + [jax.ShapeDtypeStruct((inner, rows), jnp.bfloat16)] * 3
@@ -216,15 +212,14 @@
         scratch_shapes=[
             pltpu.VMEM((2 * inner, rows), jnp.bfloat16),
             pltpu.VMEM((2 * inner, width), jnp.bfloat16),
-            pltpu.VMEM((inner, width), jnp.bfloat16),
             pltpu.VMEM((rows, width), jnp.float32),
-            pltpu.SemaphoreType.DMA((3, len(cuts))),
+            pltpu.SemaphoreType.DMA((2, len(cuts))),
         ],
         compiler_params=pltpu.CompilerParams(vmem_limit_bytes=SIGNAL_MIB << 20),
         cost_estimate=pl.CostEstimate(
             flops=6 * inner * width * rows, bytes_accessed=6 * inner * width, transcendentals=inner * rows
         ),
-    )(perm, back, *parts, pg, pu, wg, wu, wd)
+    )(perm, back, *parts, pg, pu, wd, wg, wu)
 
 
 def weight_kernel(cuts, x_ref, g_ref, out_hbm, buf_ref, sems):
@@ -338,7 +333,8 @@
     t, pg, held_s = tie((t, pg, held_s))
     got_s = send(held_s, bits - 1)
     pu = up_call(t, wu_here)
-    pu, held_s, got_s = tie((pu, held_s, got_s))
+    pu, wd = tie((pu, wd))
+    pu, held_s, got_s, wd = tie((pu, held_s, got_s, load_call(wd, 0)))
     parts_s = (held_s[0], got_s[0], held_s[1], got_s[1])
     s, h, gs, us, keepa, senda, keepb, sendb = signal_call(perm, back, parts_s, pg, pu, wg, wu, wd)
 

time: 112 us -> 113 us (level)
  Pallas kernels: 44.2 us -> 47.1 us
  waiting for transfers between devices: 27 us -> 24.7 us
    pallas_call x2 -> x3, Pallas kernels: 8.64 us -> 13 us  [load_call(): pl.pallas_call(functools.partial(load_kernel, cuts), in_specs=[pl.BlockSp...]
    ppermute x27, waiting for transfers between devices: 27 us -> 24.7 us  [swap(): lax.ppermute(value, axis, [(i, i ^ offset) for i in range(size)])[:rows]]
    pallas_call x1, Pallas kernels: 14.4 us -> 12.7 us  [signal_call(): pl.pallas_call(functools.partial(signal_kernel, cuts), in_specs=[vmem] *...]
  transfers between devices with their start and end apart: 27 -> 27, of which waited for: 17 -> 13; matrix products, arithmetic and copies ran while one was open for 3% -> 3% of each run, Pallas kernels for 27% -> 31%
where the time goes in v4:
time: 113 us
  Pallas kernels  47.1 us (42%)
  starting transfers between devices  32.1 us (28%)
  waiting for transfers between devices  24.7 us (22%)
  matrix products  3.38 us (3%)
  other arithmetic  2.87 us (3%)
  between operations  1.92 us (2%)
    ppermute x27, starting transfers between devices, swap(): lax.ppermute(value, axis, [(i, i ^ offset) for i in range(size)])[:rows]  32.1 us
    ppermute x27, waiting for transfers between devices, swap(): lax.ppermute(value, axis, [(i, i ^ offset) for i in range(size)])[:rows]  24.7 us
    pallas_call x3, Pallas kernels, weight_call(): pl.pallas_call(functools.partial(weight_kernel, cuts), in_specs=[pl.Block...  15.1 us
    pallas_call x3, Pallas kernels, load_call(): pl.pallas_call(functools.partial(load_kernel, cuts), in_specs=[pl.BlockSp...  13 us
    pallas_call x1, Pallas kernels, signal_call(): pl.pallas_call(functools.partial(signal_kernel, cuts), in_specs=[vmem] *...  12.7 us
    pallas_call x1, Pallas kernels, gate_call(): pl.pallas_call(functools.partial(gate_kernel, cuts_of(inner, STEP)), in_s...  3.23 us
    pallas_call x1, Pallas kernels, up_call(): pl.pallas_call(functools.partial(up_kernel, cuts_of(inner, STEP)), in_spe...  3.08 us
  transfers between devices with their start and end apart: 27, of which 13 were waited for; matrix products, arithmetic and copies ran while one was open for 3% of the time, Pallas kernels for 31%

profile of v4, /device:TPU:0, one launch (start us, length us, event | category | flops | bytes accessed | tf_op | source)
XLA Modules:
  0.0 112.6 jit_solution(7637531813283052163)
XLA Ops:
  3.6 2.6 %collective-permute-start.1 = (bf16[8,4096]{1,0:T(8,128)(2,1)S(1)}, bf16[8,4096]{1,0:T(8,128)(2,1)S(1)}, u32[]{:S(2)}, u32[]{:S(2)}) collective-permute-start(bf16[8,4096]{1,0:T(8,128)(2,1)S(1)} %concatenate.79), channel_id=1, source_target_pairs={{0,16},{8,24},{16,0},{24,8},{1,17},{9,25},{17,1},{25,9},{2,18},{10... | collective-permute-start | bytes 196616 | tf_op jit(solution)/shard_map/ppermute | solution.py:265
  9.0 2.0 %collective-permute-start.8 = (bf16[8,4096]{1,0:T(8,128)(2,1)S(1)}, bf16[8,4096]{1,0:T(8,128)(2,1)S(1)}, u32[]{:S(2)}, u32[]{:S(2)}) collective-permute-start(bf16[8,4096]{1,0:T(8,128)(2,1)S(1)} %concatenate.89), channel_id=1, source_target_pairs={{0,16},{8,24},{16,0},{24,8},{1,17},{9,25},{17,1},{25,9},{2,18},{10... | collective-permute-start | bytes 196616 | tf_op jit(solution)/shard_map/ppermute | solution.py:265
  13.0 2.6 %collective-permute-start.3 = (bf16[24,2048]{1,0:T(8,128)(2,1)S(1)}, bf16[24,2048]{1,0:T(8,128)(2,1)S(1)}, u32[]{:S(2)}, u32[]{:S(2)}) collective-permute-start(bf16[24,2048]{1,0:T(8,128)(2,1)S(1)} %concatenate.82), channel_id=1, source_target_pairs={{0,4},{1,5},{2,6},{3,7},{4,0},{5,1},{6,2},{7,3},{8,12},{9,13},{10,... | collective-permute-start | bytes 294920 | tf_op jit(solution)/shard_map/ppermute | solution.py:265
  15.7 4.3 %shard_map.129.wg_ref = bf16[1376,4096]{1,0:T(8,128)(2,1)S(1)} custom-call(bf16[1376,4096]{1,0:T(8,128)(2,1)} %bitcast.62), custom_call_target="tpu_custom_call" | custom-call | bytes 11272192 | tf_op jit(solution)/shard_map/pallas_call | solution.py:89
  21.8 3.4 %collective-permute-start.6 = (bf16[40,2048]{1,0:T(8,128)(2,1)S(1)}, bf16[40,2048]{1,0:T(8,128)(2,1)S(1)}, u32[]{:S(2)}, u32[]{:S(2)}) collective-permute-start(bf16[40,2048]{1,0:T(8,128)(2,1)S(1)} %pad_maximum_fusion.7), channel_id=1, source_target_pairs={{0,4},{1,5},{2,6},{3,7},{4,0},{5,1},{6,2},{7,3},{8,12},{9,13},{10,... | collective-permute-start | bytes 491528 | tf_op jit(solution)/shard_map/ppermute | solution.py:265
  25.2 4.3 %shard_map.130.wu_ref = bf16[1376,4096]{1,0:T(8,128)(2,1)S(1)} custom-call(bf16[1376,4096]{1,0:T(8,128)(2,1)} %bitcast.64), custom_call_target="tpu_custom_call" | custom-call | bytes 11272192 | tf_op jit(solution)/shard_map/pallas_call | solution.py:89
  29.8 3.1 %collective-permute-done.6 = bf16[40,2048]{1,0:T(8,128)(2,1)S(1)} collective-permute-done((bf16[40,2048]{1,0:T(8,128)(2,1)S(1)}, bf16[40,2048]{1,0:T(8,128)(2,1)S(1)}, u32[]{:S(2)}, u32[]{:S(2)}) %collective-permute-start.6) | collective-permute-done | bytes 163872 | tf_op jit(solution)/shard_map/ppermute | solution.py:265
  35.2 2.9 %collective-permute-start.11 = (bf16[80,2048]{1,0:T(8,128)(2,1)S(1)}, bf16[80,2048]{1,0:T(8,128)(2,1)S(1)}, u32[]{:S(2)}, u32[]{:S(2)}) collective-permute-start(bf16[80,2048]{1,0:T(8,128)(2,1)S(1)} %pad_maximum_fusion.1.b0_ref), channel_id=1, source_target_pairs={{0,2},{1,3},{2,0},{3,1},{4,6},{5,7},{6,4},{7,5},{8,10},{9,11},{10,... | collective-permute-start | bytes 983048 | tf_op jit(solution)/shard_map/ppermute | solution.py:265
  40.5 3.1 %collective-permute-done.10.a1_ref = bf16[80,2048]{1,0:T(8,128)(2,1)S(1)} collective-permute-done((bf16[80,2048]{1,0:T(8,128)(2,1)S(1)}, bf16[80,2048]{1,0:T(8,128)(2,1)S(1)}, u32[]{:S(2)}, u32[]{:S(2)}) %collective-permute-start.10) | collective-permute-done | bytes 327712 | tf_op jit(solution)/shard_map/ppermute | solution.py:265
  43.6 1.8 %collective-permute-done.11.b1_ref = bf16[80,2048]{1,0:T(8,128)(2,1)S(1)} collective-permute-done((bf16[80,2048]{1,0:T(8,128)(2,1)S(1)}, bf16[80,2048]{1,0:T(8,128)(2,1)S(1)}, u32[]{:S(2)}, u32[]{:S(2)}) %collective-permute-start.11) | collective-permute-done | bytes 327712 | tf_op jit(solution)/shard_map/ppermute | solution.py:265
  46.0 2.4 %collective-permute-start.15 = (bf16[40,2048]{1,0:T(8,128)(2,1)S(1)}, bf16[40,2048]{1,0:T(8,128)(2,1)S(1)}, u32[]{:S(2)}, u32[]{:S(2)}) collective-permute-start(bf16[40,2048]{1,0:T(8,128)(2,1)S(1)} %pad_maximum_fusion.9), channel_id=1, source_target_pairs={{0,4},{1,5},{2,6},{3,7},{4,0},{5,1},{6,2},{7,3},{8,12},{9,13},{10,... | collective-permute-start | bytes 491528 | tf_op jit(solution)/shard_map/ppermute | solution.py:265
  48.4 3.2 %shard_map.131 = (bf16[160,4096]{1,0:T(8,128)(2,1)S(1)}, f32[1376,160]{1,0:T(8,128)S(1)}) custom-call(bf16[160,160]{1,0:T(8,128)(2,1)S(1)} %copy-done.2, bf16[80,2048]{1,0:T(8,128)(2,1)S(1)} %pad_maximum_fusion.a0_ref, bf16[80,2048]{1,0:T(8,128)(2,1)S(1)} %collective-permute-done.10.a1_ref, bf16[80,2048]{1,0:T(8,128)(2,1)S(1)} %pad_maximum_fusion.1.b0_ref, ...), custom_call_target="tpu_custom_call" | custom-call | flops 1803550720 | bytes 11272192 | tf_op jit(solution)/shard_map/pallas_call | solution.py:110
  52.7 2.6 %collective-permute-done.15 = bf16[40,2048]{1,0:T(8,128)(2,1)S(1)} collective-permute-done((bf16[40,2048]{1,0:T(8,128)(2,1)S(1)}, bf16[40,2048]{1,0:T(8,128)(2,1)S(1)}, u32[]{:S(2)}, u32[]{:S(2)}) %collective-permute-start.15) | collective-permute-done | bytes 163872 | tf_op jit(solution)/shard_map/ppermute | solution.py:265
  56.2 3.1 %shard_map.132.pu_ref = f32[1376,160]{1,0:T(8,128)S(1)} custom-call(bf16[160,4096]{1,0:T(8,128)(2,1)S(1)} %get-tuple-element.116.t_ref.x_ref, bf16[1376,4096]{1,0:T(8,128)(2,1)S(1)} %shard_map.130.wu_ref), custom_call_target="tpu_custom_call" | custom-call | flops 1803550720 | bytes 11272192 | tf_op jit(solution)/shard_map/pallas_call | solution.py:134
  59.3 4.3 %shard_map.133.wd_ref = bf16[1376,4096]{1,0:T(8,128)(2,1)S(1)} custom-call(bf16[1376,4096]{1,0:T(8,128)(2,1)} %bitcast.69), custom_call_target="tpu_custom_call" | custom-call | bytes 11272192 | tf_op jit(solution)/shard_map/pallas_call | solution.py:89
  63.6 12.7 %shard_map.134 = (bf16[160,4096]{1,0:T(8,128)(2,1)S(1)}, bf16[1376,160]{1,0:T(8,128)(2,1)S(1)}, bf16[1376,160]{1,0:T(8,128)(2,1)S(1)}, bf16[1376,160]{1,0:T(8,12...) custom-call(bf16[160,160]{1,0:T(8,128)(2,1)S(1)} %copy-done.2, ...), custom_call_target="tpu_custom_call" | custom-call | flops 5410652160 | bytes 33816576 | tf_op jit(solution)/shard_map/pallas_call | solution.py:205
  77.8 2.0 %collective-permute-start.19 = (bf16[80,2048]{1,0:T(8,128)(2,1)S(1)}, bf16[80,2048]{1,0:T(8,128)(2,1)S(1)}, u32[]{:S(2)}, u32[]{:S(2)}) collective-permute-start(bf16[80,2048]{1,0:T(8,128)(2,1)S(1)} %get-tuple-element.107), channel_id=1, source_target_pairs={{0,2},{1,3},{2,0},{3,1},{4,6},{5,7},{6,4},{7,5},{8,10},{9,11},{10,... | collective-permute-start | bytes 983048 | tf_op jit(solution)/shard_map/ppermute | solution.py:265
  79.8 4.9 %shard_map.136 = bf16[1376,4096]{1,0:T(8,128)(2,1)} custom-call(bf16[160,4096]{1,0:T(8,128)(2,1)S(1)} %get-tuple-element.116.t_ref.x_ref, bf16[1376,160]{1,0:T(8,128)(2,1)S(1)} %get-tuple-element.110.g_ref), custom_call_target="tpu_custom_call" | custom-call | flops 1803550720 | bytes 11272192 | tf_op jit(solution)/shard_map/pallas_call | solution.py:247
  84.7 5.0 %shard_map.135 = bf16[1376,4096]{1,0:T(8,128)(2,1)} custom-call(bf16[160,4096]{1,0:T(8,128)(2,1)S(1)} %get-tuple-element.108.x_ref, bf16[1376,160]{1,0:T(8,128)(2,1)S(1)} %get-tuple-element.109.g_ref), custom_call_target="tpu_custom_call" | custom-call | flops 1803550720 | bytes 11272192 | tf_op jit(solution)/shard_map/pallas_call | solution.py:247
  90.6 2.0 %collective-permute-start.20 = (bf16[40,2048]{1,0:T(8,128)(2,1)S(1)}, bf16[40,2048]{1,0:T(8,128)(2,1)S(1)}, u32[]{:S(2)}, u32[]{:S(2)}) collective-permute-start(bf16[40,2048]{1,0:T(8,128)(2,1)S(1)} %slice.146), channel_id=1, source_target_pairs={{0,2},{1,3},{2,0},{3,1},{4,6},{5,7},{6,4},{7,5},{8,10},{9,11},{10,... | collective-permute-start | bytes 491528 | tf_op jit(solution)/shard_map/ppermute | solution.py:265
  92.6 5.2 %shard_map.137 = bf16[1376,4096]{1,0:T(8,128)(2,1)} custom-call(bf16[160,4096]{1,0:T(8,128)(2,1)S(1)} %get-tuple-element.116.t_ref.x_ref, bf16[1376,160]{1,0:T(8,128)(2,1)S(1)} %get-tuple-element.117.g_ref), custom_call_target="tpu_custom_call" | custom-call | flops 1803550720 | bytes 11272192 | tf_op jit(solution)/shard_map/pallas_call | solution.py:247
  99.2 3.5 %collective-permute-done.23 = bf16[24,2048]{1,0:T(8,128)(2,1)S(1)} collective-permute-done((bf16[24,2048]{1,0:T(8,128)(2,1)S(1)}, bf16[24,2048]{1,0:T(8,128)(2,1)S(1)}, u32[]{:S(2)}, u32[]{:S(2)}) %collective-permute-start.23) | collective-permute-done | bytes 98336 | tf_op jit(solution)/shard_map/ppermute | solution.py:265
  102.7 2.3 %collective-permute-done.22 = bf16[24,2048]{1,0:T(8,128)(2,1)S(1)} collective-permute-done((bf16[24,2048]{1,0:T(8,128)(2,1)S(1)}, bf16[24,2048]{1,0:T(8,128)(2,1)S(1)}, u32[]{:S(2)}, u32[]{:S(2)}) %collective-permute-start.22) | collective-permute-done | bytes 98336 | tf_op jit(solution)/shard_map/ppermute | solution.py:265
  107.2 2.8 %collective-permute-done.25 = bf16[8,4096]{1,0:T(8,128)(2,1)S(1)} collective-permute-done((bf16[8,4096]{1,0:T(8,128)(2,1)S(1)}, bf16[8,4096]{1,0:T(8,128)(2,1)S(1)}, u32[]{:S(2)}, u32[]{:S(2)}) %collective-permute-start.25) | collective-permute-done | bytes 65568 | tf_op jit(solution)/shard_map/ppermute | solution.py:265
  (106 shorter events, 24.6 us)
Async XLA Ops:
  3.0 8.1 %collective-permute-start = (bf16[8,4096]{1,0:T(8,128)(2,1)S(1)}, bf16[8,4096]{1,0:T(8,128)(2,1)S(1)}, u32[]{:S(2)}, u32[]{:S(2)}) collective-permute-start(bf16[8,4096]{1,0:T(8,128)(2,1)S(1)} %concatenate.78), channel_id=1, source_target_pairs={{0,8},{8,0},{16,24},{24,16},{1,9},{9,1},{17,25},{25,17},{2,10},{10... | collective-permute-start | bytes 196616 | tf_op jit(solution)/shard_map/ppermute | solution.py:265
  3.6 7.6 %collective-permute-start.1 = (bf16[8,4096]{1,0:T(8,128)(2,1)S(1)}, bf16[8,4096]{1,0:T(8,128)(2,1)S(1)}, u32[]{:S(2)}, u32[]{:S(2)}) collective-permute-start(bf16[8,4096]{1,0:T(8,128)(2,1)S(1)} %concatenate.79), channel_id=1, source_target_pairs={{0,16},{8,24},{16,0},{24,8},{1,17},{9,25},{17,1},{25,9},{2,18},{10... | collective-permute-start | bytes 196616 | tf_op jit(solution)/shard_map/ppermute | solution.py:265
  6.1 5.0 %collective-permute-start.2 = (bf16[8,4096]{1,0:T(8,128)(2,1)S(1)}, bf16[8,4096]{1,0:T(8,128)(2,1)S(1)}, u32[]{:S(2)}, u32[]{:S(2)}) collective-permute-start(bf16[8,4096]{1,0:T(8,128)(2,1)S(1)} %concatenate.80), channel_id=1, source_target_pairs={{0,24},{8,16},{16,8},{24,0},{1,25},{9,17},{17,9},{25,1},{2,26},{10... | collective-permute-start | bytes 196616 | tf_op jit(solution)/shard_map/ppermute | solution.py:265
  8.8 6.7 %collective-permute-start.7 = (bf16[8,4096]{1,0:T(8,128)(2,1)S(1)}, bf16[8,4096]{1,0:T(8,128)(2,1)S(1)}, u32[]{:S(2)}, u32[]{:S(2)}) collective-permute-start(bf16[8,4096]{1,0:T(8,128)(2,1)S(1)} %concatenate.88), channel_id=1, source_target_pairs={{0,8},{8,0},{16,24},{24,16},{1,9},{9,1},{17,25},{25,17},{2,10},{10... | collective-permute-start | bytes 196616 | tf_op jit(solution)/shard_map/ppermute | solution.py:265
  9.0 6.5 %collective-permute-start.8 = (bf16[8,4096]{1,0:T(8,128)(2,1)S(1)}, bf16[8,4096]{1,0:T(8,128)(2,1)S(1)}, u32[]{:S(2)}, u32[]{:S(2)}) collective-permute-start(bf16[8,4096]{1,0:T(8,128)(2,1)S(1)} %concatenate.89), channel_id=1, source_target_pairs={{0,16},{8,24},{16,0},{24,8},{1,17},{9,25},{17,1},{25,9},{2,18},{10... | collective-permute-start | bytes 196616 | tf_op jit(solution)/shard_map/ppermute | solution.py:265
  11.3 8.7 %collective-permute-start.4 = (bf16[24,2048]{1,0:T(8,128)(2,1)S(1)}, bf16[24,2048]{1,0:T(8,128)(2,1)S(1)}, u32[]{:S(2)}, u32[]{:S(2)}) collective-permute-start(bf16[24,2048]{1,0:T(8,128)(2,1)S(1)} %concatenate.84), channel_id=1, source_target_pairs={{0,1},{1,0},{2,3},{3,2},{4,5},{5,4},{6,7},{7,6},{8,9},{9,8},{10,11... | collective-permute-start | bytes 294920 | tf_op jit(solution)/shard_map/ppermute | solution.py:265
  13.0 8.0 %collective-permute-start.3 = (bf16[24,2048]{1,0:T(8,128)(2,1)S(1)}, bf16[24,2048]{1,0:T(8,128)(2,1)S(1)}, u32[]{:S(2)}, u32[]{:S(2)}) collective-permute-start(bf16[24,2048]{1,0:T(8,128)(2,1)S(1)} %concatenate.82), channel_id=1, source_target_pairs={{0,4},{1,5},{2,6},{3,7},{4,0},{5,1},{6,2},{7,3},{8,12},{9,13},{10,... | collective-permute-start | bytes 294920 | tf_op jit(solution)/shard_map/ppermute | solution.py:265
  21.0 8.8 %collective-permute-start.5 = (bf16[40,2048]{1,0:T(8,128)(2,1)S(1)}, bf16[40,2048]{1,0:T(8,128)(2,1)S(1)}, u32[]{:S(2)}, u32[]{:S(2)}) collective-permute-start(bf16[40,2048]{1,0:T(8,128)(2,1)S(1)} %pad_maximum_fusion.6), channel_id=1, source_target_pairs={{0,2},{1,3},{2,0},{3,1},{4,6},{5,7},{6,4},{7,5},{8,10},{9,11},{10,... | collective-permute-start | bytes 491528 | tf_op jit(solution)/shard_map/ppermute | solution.py:265
  21.8 11.1 %collective-permute-start.6 = (bf16[40,2048]{1,0:T(8,128)(2,1)S(1)}, bf16[40,2048]{1,0:T(8,128)(2,1)S(1)}, u32[]{:S(2)}, u32[]{:S(2)}) collective-permute-start(bf16[40,2048]{1,0:T(8,128)(2,1)S(1)} %pad_maximum_fusion.7), channel_id=1, source_target_pairs={{0,4},{1,5},{2,6},{3,7},{4,0},{5,1},{6,2},{7,3},{8,12},{9,13},{10,... | collective-permute-start | bytes 491528 | tf_op jit(solution)/shard_map/ppermute | solution.py:265
  32.9 5.7 %collective-permute-start.13 = (bf16[24,2048]{1,0:T(8,128)(2,1)S(1)}, bf16[24,2048]{1,0:T(8,128)(2,1)S(1)}, u32[]{:S(2)}, u32[]{:S(2)}) collective-permute-start(bf16[24,2048]{1,0:T(8,128)(2,1)S(1)} %concatenate.94), channel_id=1, source_target_pairs={{0,1},{1,0},{2,3},{3,2},{4,5},{5,4},{6,7},{7,6},{8,9},{9,8},{10,11... | collective-permute-start | bytes 294920 | tf_op jit(solution)/shard_map/ppermute | solution.py:265
  33.8 6.6 %collective-permute-start.12 = (bf16[24,2048]{1,0:T(8,128)(2,1)S(1)}, bf16[24,2048]{1,0:T(8,128)(2,1)S(1)}, u32[]{:S(2)}, u32[]{:S(2)}) collective-permute-start(bf16[24,2048]{1,0:T(8,128)(2,1)S(1)} %concatenate.92), channel_id=1, source_target_pairs={{0,4},{1,5},{2,6},{3,7},{4,0},{5,1},{6,2},{7,3},{8,12},{9,13},{10,... | collective-permute-start | bytes 294920 | tf_op jit(solution)/shard_map/ppermute | solution.py:265
  34.1 9.4 %collective-permute-start.10 = (bf16[80,2048]{1,0:T(8,128)(2,1)S(1)}, bf16[80,2048]{1,0:T(8,128)(2,1)S(1)}, u32[]{:S(2)}, u32[]{:S(2)}) collective-permute-start(bf16[80,2048]{1,0:T(8,128)(2,1)S(1)} %pad_maximum_fusion.a0_ref), channel_id=1, source_target_pairs={{0,1},{1,0},{2,3},{3,2},{4,5},{5,4},{6,7},{7,6},{8,9},{9,8},{10,11... | collective-permute-start | bytes 983048 | tf_op jit(solution)/shard_map/ppermute | solution.py:265
  35.2 10.1 %collective-permute-start.11 = (bf16[80,2048]{1,0:T(8,128)(2,1)S(1)}, bf16[80,2048]{1,0:T(8,128)(2,1)S(1)}, u32[]{:S(2)}, u32[]{:S(2)}) collective-permute-start(bf16[80,2048]{1,0:T(8,128)(2,1)S(1)} %pad_maximum_fusion.1.b0_ref), channel_id=1, source_target_pairs={{0,2},{1,3},{2,0},{3,1},{4,6},{5,7},{6,4},{7,5},{8,10},{9,11},{10,... | collective-permute-start | bytes 983048 | tf_op jit(solution)/shard_map/ppermute | solution.py:265
  45.3 7.3 %collective-permute-start.14 = (bf16[40,2048]{1,0:T(8,128)(2,1)S(1)}, bf16[40,2048]{1,0:T(8,128)(2,1)S(1)}, u32[]{:S(2)}, u32[]{:S(2)}) collective-permute-start(bf16[40,2048]{1,0:T(8,128)(2,1)S(1)} %pad_maximum_fusion.8), channel_id=1, source_target_pairs={{0,2},{1,3},{2,0},{3,1},{4,6},{5,7},{6,4},{7,5},{8,10},{9,11},{10,... | collective-permute-start | bytes 491528 | tf_op jit(solution)/shard_map/ppermute | solution.py:265
  46.0 9.3 %collective-permute-start.15 = (bf16[40,2048]{1,0:T(8,128)(2,1)S(1)}, bf16[40,2048]{1,0:T(8,128)(2,1)S(1)}, u32[]{:S(2)}, u32[]{:S(2)}) collective-permute-start(bf16[40,2048]{1,0:T(8,128)(2,1)S(1)} %pad_maximum_fusion.9), channel_id=1, source_target_pairs={{0,4},{1,5},{2,6},{3,7},{4,0},{5,1},{6,2},{7,3},{8,12},{9,13},{10,... | collective-permute-start | bytes 491528 | tf_op jit(solution)/shard_map/ppermute | solution.py:265
  55.4 8.2 %collective-permute-start.16 = (bf16[80,2048]{1,0:T(8,128)(2,1)S(1)}, bf16[80,2048]{1,0:T(8,128)(2,1)S(1)}, u32[]{:S(2)}, u32[]{:S(2)}) collective-permute-start(bf16[80,2048]{1,0:T(8,128)(2,1)S(1)} %pad_maximum_fusion.2.a0_ref), channel_id=1, source_target_pairs={{0,1},{1,0},{2,3},{3,2},{4,5},{5,4},{6,7},{7,6},{8,9},{9,8},{10,11... | collective-permute-start | bytes 983048 | tf_op jit(solution)/shard_map/ppermute | solution.py:265
  56.1 7.5 %collective-permute-start.17 = (bf16[80,2048]{1,0:T(8,128)(2,1)S(1)}, bf16[80,2048]{1,0:T(8,128)(2,1)S(1)}, u32[]{:S(2)}, u32[]{:S(2)}) collective-permute-start(bf16[80,2048]{1,0:T(8,128)(2,1)S(1)} %pad_maximum_fusion.3.b0_ref), channel_id=1, source_target_pairs={{0,2},{1,3},{2,0},{3,1},{4,6},{5,7},{6,4},{7,5},{8,10},{9,11},{10,... | collective-permute-start | bytes 983048 | tf_op jit(solution)/shard_map/ppermute | solution.py:265
  76.4 13.3 %collective-permute-start.18 = (bf16[80,2048]{1,0:T(8,128)(2,1)S(1)}, bf16[80,2048]{1,0:T(8,128)(2,1)S(1)}, u32[]{:S(2)}, u32[]{:S(2)}) collective-permute-start(bf16[80,2048]{1,0:T(8,128)(2,1)S(1)} %get-tuple-element.105), channel_id=1, source_target_pairs={{0,1},{1,0},{2,3},{3,2},{4,5},{5,4},{6,7},{7,6},{8,9},{9,8},{10,11... | collective-permute-start | bytes 983048 | tf_op jit(solution)/shard_map/ppermute | solution.py:265
  77.8 12.0 %collective-permute-start.19 = (bf16[80,2048]{1,0:T(8,128)(2,1)S(1)}, bf16[80,2048]{1,0:T(8,128)(2,1)S(1)}, u32[]{:S(2)}, u32[]{:S(2)}) collective-permute-start(bf16[80,2048]{1,0:T(8,128)(2,1)S(1)} %get-tuple-element.107), channel_id=1, source_target_pairs={{0,2},{1,3},{2,0},{3,1},{4,6},{5,7},{6,4},{7,5},{8,10},{9,11},{10,... | collective-permute-start | bytes 983048 | tf_op jit(solution)/shard_map/ppermute | solution.py:265
  89.9 7.9 %collective-permute-start.21 = (bf16[40,2048]{1,0:T(8,128)(2,1)S(1)}, bf16[40,2048]{1,0:T(8,128)(2,1)S(1)}, u32[]{:S(2)}, u32[]{:S(2)}) collective-permute-start(bf16[40,2048]{1,0:T(8,128)(2,1)S(1)} %slice.148), channel_id=1, source_target_pairs={{0,4},{1,5},{2,6},{3,7},{4,0},{5,1},{6,2},{7,3},{8,12},{9,13},{10,... | collective-permute-start | bytes 491528 | tf_op jit(solution)/shard_map/ppermute | solution.py:265
  90.6 7.3 %collective-permute-start.20 = (bf16[40,2048]{1,0:T(8,128)(2,1)S(1)}, bf16[40,2048]{1,0:T(8,128)(2,1)S(1)}, u32[]{:S(2)}, u32[]{:S(2)}) collective-permute-start(bf16[40,2048]{1,0:T(8,128)(2,1)S(1)} %slice.146), channel_id=1, source_target_pairs={{0,2},{1,3},{2,0},{3,1},{4,6},{5,7},{6,4},{7,5},{8,10},{9,11},{10,... | collective-permute-start | bytes 491528 | tf_op jit(solution)/shard_map/ppermute | solution.py:265
  98.0 4.7 %collective-permute-start.23 = (bf16[24,2048]{1,0:T(8,128)(2,1)S(1)}, bf16[24,2048]{1,0:T(8,128)(2,1)S(1)}, u32[]{:S(2)}, u32[]{:S(2)}) collective-permute-start(bf16[24,2048]{1,0:T(8,128)(2,1)S(1)} %concatenate.99), channel_id=1, source_target_pairs={{0,1},{1,0},{2,3},{3,2},{4,5},{5,4},{6,7},{7,6},{8,9},{9,8},{10,11... | collective-permute-start | bytes 294920 | tf_op jit(solution)/shard_map/ppermute | solution.py:265
  98.9 6.1 %collective-permute-start.22 = (bf16[24,2048]{1,0:T(8,128)(2,1)S(1)}, bf16[24,2048]{1,0:T(8,128)(2,1)S(1)}, u32[]{:S(2)}, u32[]{:S(2)}) collective-permute-start(bf16[24,2048]{1,0:T(8,128)(2,1)S(1)} %concatenate.98), channel_id=1, source_target_pairs={{0,4},{1,5},{2,6},{3,7},{4,0},{5,1},{6,2},{7,3},{8,12},{9,13},{10,... | collective-permute-start | bytes 294920 | tf_op jit(solution)/shard_map/ppermute | solution.py:265
  105.3 4.7 %collective-permute-start.25 = (bf16[8,4096]{1,0:T(8,128)(2,1)S(1)}, bf16[8,4096]{1,0:T(8,128)(2,1)S(1)}, u32[]{:S(2)}, u32[]{:S(2)}) collective-permute-start(bf16[8,4096]{1,0:T(8,128)(2,1)S(1)} %concatenate.102), channel_id=1, source_target_pairs={{0,16},{8,24},{16,0},{24,8},{1,17},{9,25},{17,1},{25,9},{2,18},{10... | collective-permute-start | bytes 196616 | tf_op jit(solution)/shard_map/ppermute | solution.py:265
  (7 other events, 66.8 us)
